TPU v7x, 256 devices: a whole 4x4x8 slice. The times are simulated.
256 devices in a mesh: pipe: 8 (over z_hi, y), expert: 8 (over z_lo, core), dp: 4 (over x).
Axes of the slice: x: 4, y: 4, z: 8 (z_hi: 2, z_lo: 4; z = z_hi * 4 + z_lo), core: 2. Of those that a mesh axis runs over, the one named last changes fastest.
Arguments:
- adjoint_out: bfloat16 [4096, 2048], P(('expert', 'dp')), may hold values from -6 to 6
- gate_probs: float32 [8, 4096, 2], P('pipe', ('expert', 'dp')), may hold values from 0.2 to 0.8
- routes: int32 [8, 4096, 2], P('pipe', ('expert', 'dp')), may hold values from 0 to 7, all different within a row; in each aligned block of 16 rows (0 to 15, 16 to 31, ..., all dimensions but the last counted through in order) at most 6 rows name the same one
- saved: bfloat16 [8, 8, 4, 8, 4, 48, 512], P('pipe', 'expert', 'dp'), may hold values from -6 to 6
- w_gate: bfloat16 [8, 8, 2048, 512], P('pipe', 'expert'), may hold values from -0.25 to 0.25
- w_up: bfloat16 [8, 8, 2048, 512], P('pipe', 'expert'), may hold values from -0.25 to 0.25
- w_down: bfloat16 [8, 8, 512, 2048], P('pipe', 'expert'), may hold values from -0.125 to 0.125
- probe: bfloat16 [8, 8, 2048, 512], P('pipe', 'expert'), may hold values from -0.125 to 0.125
Outputs:
- curvature_diag: float32 [8, 8, 2048, 512], P('pipe', 'expert', 'dp')
Inputs may be any that keep to these rules, and one draw needn't show every extreme that they name: `routes`: each row names 2 different experts. In each block of 16 rows of one section (one microbatch of one device) no expert is named by more than 6 rows, and in some blocks one expert is named by exactly 6.
All inputs are finite; a program needn't handle non-finite values.
Results may differ from a plain program's by a relative error of at most 0.025.
Values may be sent and summed in bfloat16 or wider, within the bound.
A program may use at most 64 MiB of HBM per device.

v0:
```python
import jax
import jax.numpy as jnp
from jax import lax
from jax.sharding import PartitionSpec as P

TOP = 2
T_MB = 16
M = 8


def passed_along(value, axis, steps):
    count = lax.axis_size(axis)
    first, last = (max(0, -steps), min(count, count - steps))
    return lax.ppermute(value, axis, [(source, source + steps) for source in range(first, last)])


def contract_last(left, right):
    return lax.dot_general(
        left, right, (((1,), (1,)), ((), ())), preferred_element_type=jnp.float32
    )


def contract_first(left, right):
    return lax.dot_general(
        left, right, (((0,), (0,)), ((), ())), preferred_element_type=jnp.float32
    )


def expert_terms(pre_acts, adjoint_rows, tangent_rows, w_down, probe):
    pre_gate = pre_acts[0].astype(jnp.float32)
    pre_up = pre_acts[1].astype(jnp.float32)
    tangent_gate = pre_acts[2].astype(jnp.float32)
    tangent_up = pre_acts[3].astype(jnp.float32)
    gate_sigmoid = jax.nn.sigmoid(pre_gate)
    silu_out = pre_gate * gate_sigmoid
    first_slope = gate_sigmoid * (1.0 + pre_gate * (1.0 - gate_sigmoid))
    second_slope = (
        gate_sigmoid * (1.0 - gate_sigmoid) * (2.0 + pre_gate * (1.0 - 2.0 * gate_sigmoid))
    )
    hidden = (silu_out * pre_up).astype(jnp.bfloat16)
    hidden_dot = (first_slope * tangent_gate * pre_up + silu_out * tangent_up).astype(jnp.bfloat16)
    grad_hidden = contract_last(adjoint_rows, w_down)
    grad_hidden_dot = contract_last(tangent_rows, w_down) + jnp.dot(
        adjoint_rows, probe, preferred_element_type=jnp.float32
    )
    grad_gate = (grad_hidden * pre_up * first_slope).astype(jnp.bfloat16)
    grad_up = (grad_hidden * silu_out).astype(jnp.bfloat16)
    grad_gate_dot = (
        grad_hidden_dot * pre_up * first_slope
        + grad_hidden * tangent_up * first_slope
        + grad_hidden * pre_up * second_slope * tangent_gate
    ).astype(jnp.bfloat16)
    grad_up_dot = (grad_hidden_dot * silu_out + grad_hidden * first_slope * tangent_gate).astype(
        jnp.bfloat16
    )
    return (hidden, hidden_dot, grad_gate, grad_up, grad_gate_dot, grad_up_dot)


def input_grads(grad_gate, grad_up, w_gate, w_up):
    return (contract_last(grad_gate, w_gate) + contract_last(grad_up, w_up)).astype(jnp.bfloat16)


def per_device(adjoint_out, gate_probs, routes, saved, w_gate, w_up, w_down, probe):
    section_count = lax.axis_size("pipe")
    section_index = lax.axis_index("pipe")
    group_count = lax.axis_size("expert")
    slot_count = saved.shape[5]
    capacity = slot_count // group_count
    model_width = adjoint_out.shape[1]
    hidden_width = w_gate.shape[3]
    turn_count = M + section_count - 1
    pre_all = saved[0, 0, 0]
    gate_local = w_gate[0, 0]
    up_local = w_up[0, 0]
    down_local = w_down[0, 0]
    probe_local = probe[0, 0]
    route_rows = routes[0]
    prob_rows = gate_probs[0]
    slot_lanes = jnp.arange(group_count * capacity, dtype=jnp.int32)
    expert_ids = jnp.arange(group_count, dtype=jnp.int32)

    def advance(turn_index, loop_state):
        (
            adjoint_prev,
            tangent_prev,
            adjoint_history,
            tangent_history,
            hidden_history,
            hidden_dot_history,
        ) = loop_state
        micro_now = turn_index - (section_count - 1 - section_index)
        is_live = jnp.logical_and(micro_now >= 0, micro_now < M)
        micro_clip = jnp.clip(micro_now, 0, M - 1)
        row_start = micro_clip * T_MB
        fresh_rows = lax.dynamic_slice_in_dim(adjoint_out, row_start, T_MB, 0)
        is_last = section_index == section_count - 1
        adjoint_now = jnp.where(is_last, fresh_rows, adjoint_prev)
        tangent_now = jnp.where(is_last, jnp.zeros_like(tangent_prev), tangent_prev)
        adjoint_now = jnp.where(is_live, adjoint_now, jnp.zeros_like(adjoint_now))
        tangent_now = jnp.where(is_live, tangent_now, jnp.zeros_like(tangent_now))
        chosen = lax.dynamic_slice_in_dim(route_rows, row_start, T_MB, 0)
        weights = lax.dynamic_slice_in_dim(prob_rows, row_start, T_MB, 0)
        onehot = (
            (chosen[:, :, None] == expert_ids).astype(jnp.int32).reshape(T_MB * TOP, group_count)
        )
        before = jnp.cumsum(onehot, axis=0) - onehot
        position = jnp.sum(before * onehot, axis=1)
        target = chosen.reshape(-1) * capacity + position
        placing = (target[:, None] == slot_lanes[None, :]).astype(jnp.bfloat16)
        adjoint_pick = (
            (weights[:, :, None] * adjoint_now.astype(jnp.float32)[:, None, :])
            .astype(jnp.bfloat16)
            .reshape(-1, model_width)
        )
        tangent_pick = (
            (weights[:, :, None] * tangent_now.astype(jnp.float32)[:, None, :])
            .astype(jnp.bfloat16)
            .reshape(-1, model_width)
        )
        send_adjoint = (
            contract_first(placing, adjoint_pick)
            .astype(jnp.bfloat16)
            .reshape(group_count, capacity, model_width)
        )
        send_tangent = (
            contract_first(placing, tangent_pick)
            .astype(jnp.bfloat16)
            .reshape(group_count, capacity, model_width)
        )
        recv_adjoint, recv_tangent = (
            lax.all_to_all(send_adjoint, "expert", split_axis=0, concat_axis=0, tiled=True),
            lax.all_to_all(send_tangent, "expert", split_axis=0, concat_axis=0, tiled=True),
        )
        recv_adjoint = recv_adjoint.reshape(slot_count, model_width)
        recv_tangent = recv_tangent.reshape(slot_count, model_width)
        pre_now = lax.dynamic_index_in_dim(pre_all, micro_clip, 0, keepdims=False)
        hidden, hidden_dot, grad_gate, grad_up, grad_gate_dot, grad_up_dot = expert_terms(
            pre_now, recv_adjoint, recv_tangent, down_local, probe_local
        )
        back_adjoint = input_grads(grad_gate, grad_up, gate_local, up_local).reshape(
            group_count, capacity, model_width
        )
        back_tangent = input_grads(grad_gate_dot, grad_up_dot, gate_local, up_local).reshape(
            group_count, capacity, model_width
        )
        returned, returned_dot = (
            lax.all_to_all(back_adjoint, "expert", split_axis=0, concat_axis=0, tiled=True),
            lax.all_to_all(back_tangent, "expert", split_axis=0, concat_axis=0, tiled=True),
        )
        returned = returned.reshape(-1, model_width)
        returned_dot = returned_dot.reshape(-1, model_width)
        merge_rows = jnp.sum(placing.reshape(T_MB, TOP, -1), axis=1)
        adjoint_new = (
            adjoint_now.astype(jnp.float32)
            + jnp.dot(merge_rows, returned, preferred_element_type=jnp.float32)
        ).astype(jnp.bfloat16)
        tangent_new = (
            tangent_now.astype(jnp.float32)
            + jnp.dot(merge_rows, returned_dot, preferred_element_type=jnp.float32)
        ).astype(jnp.bfloat16)
        adjoint_next, tangent_next = passed_along((adjoint_new, tangent_new), "pipe", -1)
        adjoint_history = lax.dynamic_update_index_in_dim(
            adjoint_history, recv_adjoint, turn_index, 0
        )
        tangent_history = lax.dynamic_update_index_in_dim(
            tangent_history, recv_tangent, turn_index, 0
        )
        hidden_history = lax.dynamic_update_index_in_dim(hidden_history, hidden, turn_index, 0)
        hidden_dot_history = lax.dynamic_update_index_in_dim(
            hidden_dot_history, hidden_dot, turn_index, 0
        )
        return (
            adjoint_next,
            tangent_next,
            adjoint_history,
            tangent_history,
            hidden_history,
            hidden_dot_history,
        )

    start_state = (
        jnp.zeros((T_MB, model_width), jnp.bfloat16),
        jnp.zeros((T_MB, model_width), jnp.bfloat16),
        jnp.zeros((turn_count, slot_count, model_width), jnp.bfloat16),
        jnp.zeros((turn_count, slot_count, model_width), jnp.bfloat16),
        jnp.zeros((turn_count, slot_count, hidden_width), jnp.bfloat16),
        jnp.zeros((turn_count, slot_count, hidden_width), jnp.bfloat16),
    )
    final_state = lax.fori_loop(0, turn_count, advance, start_state)
    adjoint_rows = final_state[2].reshape(-1, model_width)
    tangent_rows = final_state[3].reshape(-1, model_width)
    hidden_rows = final_state[4].reshape(-1, hidden_width)
    hidden_dot_rows = final_state[5].reshape(-1, hidden_width)
    share_rows = model_width // lax.axis_size("dp")
    summed = lax.psum_scatter(
        (
            contract_first(adjoint_rows, hidden_dot_rows)
            + contract_first(tangent_rows, hidden_rows)
        ).astype(jnp.bfloat16),
        "dp",
        scatter_dimension=0,
        tiled=True,
    ).astype(jnp.float32)
    own_probe = lax.dynamic_slice_in_dim(
        probe_local, lax.axis_index("dp") * share_rows, share_rows, 0
    )
    return (own_probe.astype(jnp.float32) * summed)[None, None]


def solution(mesh):
    return jax.shard_map(
        per_device,
        mesh=mesh,
        in_specs=(
            P(("expert", "dp"), None),
            P("pipe", ("expert", "dp"), None),
            P("pipe", ("expert", "dp"), None),
            P("pipe", "expert", "dp", None, None, None, None),
            P("pipe", "expert", None, None),
            P("pipe", "expert", None, None),
            P("pipe", "expert", None, None),
            P("pipe", "expert", None, None),
        ),
        out_specs=P("pipe", "expert", "dp", None),
        check_vma=False,
    )
```

profile of v0, /device:TPU:1, one launch (start us, length us, event | category | flops | bytes accessed | tf_op | source)
XLA Modules:
  0.0 1179.4 jit_solution(11537866646391366462)
XLA Ops:
  8.8 1103.6 %while.27 = (s32[]{:T(128)}, bf16[16,2048]{1,0:T(8,128)(2,1)S(1)}, bf16[16,2048]{1,0:T(8,128)(2,1)S(1)}, bf16[15,48,2048]{2,1,0:T(8,128)(2,1)}, bf16[15,48,2048]...) while((s32[]{:T(128)}, bf16[16,2048]{1,0:T(8,128)(2,1)S(1)}, ...), condition=%wide.region_4.5_spmd.clone.clone, body=%wide.region_0.4_spmd.clone.clone.sunk | while | flops 726778240 | bytes 72970792 | solution.py:189
  11.5 7.5 all-to-all-start.2
  33.0 7.8 all-to-all-done
  67.7 6.4 all-to-all-done.1
  82.1 5.6 all-to-all-start.2
  101.7 7.8 all-to-all-done
  136.4 6.4 all-to-all-done.1
  150.8 5.6 all-to-all-start.2
  160.5 5.9 all-to-all-done.2
  171.3 7.8 all-to-all-done
  206.1 6.4 all-to-all-done.1
  220.4 5.6 all-to-all-start.2
  230.1 5.4 all-to-all-done.2
  235.5 5.6 all-to-all-start
  242.0 7.8 all-to-all-done
  276.7 6.4 all-to-all-done.1
  292.9 5.4 all-to-all-start.2
  302.3 6.1 all-to-all-done.2
  313.7 7.8 all-to-all-done
  348.4 6.4 all-to-all-done.1
  357.7 7.3 collective-permute-done
  377.1 6.1 all-to-all-done.2
  388.4 7.8 all-to-all-done
  423.2 6.4 all-to-all-done.1
  432.5 7.3 collective-permute-done
  451.8 6.1 all-to-all-done.2
  463.2 7.8 all-to-all-done
  497.9 6.4 all-to-all-done.1
  507.2 7.2 collective-permute-done
  526.5 6.1 all-to-all-done.2
  537.9 7.8 all-to-all-done
  572.6 6.4 all-to-all-done.1
  581.9 7.3 collective-permute-done
  601.3 6.1 all-to-all-done.2
  612.6 7.8 all-to-all-done
  647.4 6.4 all-to-all-done.1
  656.7 7.3 collective-permute-done
  666.6 5.4 all-to-all-start.2
  676.0 6.1 all-to-all-done.2
  687.4 7.8 all-to-all-done
  722.1 6.4 all-to-all-done.1
  731.4 7.3 collective-permute-done
  741.4 5.4 all-to-all-start.2
  750.8 6.1 all-to-all-done.2
  762.1 7.8 all-to-all-done
  796.9 6.4 all-to-all-done.1
  806.2 7.2 collective-permute-done
  825.5 6.1 all-to-all-done.2
  836.8 7.8 all-to-all-done
  871.6 6.4 all-to-all-done.1
  880.9 7.3 collective-permute-done
  900.2 6.1 all-to-all-done.2
  911.6 7.8 all-to-all-done
  946.3 6.4 all-to-all-done.1
  955.6 7.2 collective-permute-done
  975.0 6.1 all-to-all-done.2
  986.3 7.8 all-to-all-done
  1021.1 6.4 all-to-all-done.1
  1030.4 7.3 collective-permute-done
  1049.7 6.1 all-to-all-done.2
  1061.1 7.8 all-to-all-done
  1095.8 6.4 all-to-all-done.1
  1105.1 7.2 collective-permute-done
  1119.8 50.5 %reduce-scatter.2.cloned.1.call-done = bf16[512,512]{1,0:T(8,128)(2,1)} async-done(((bf16[2048,512]{1,0:T(8,128)(2,1)}), bf16[512,512]{1,0:T(8,128)(2,1)}) %reduce-scatter.2.cloned.1.call-update) | async-done | bytes 524304 | tf_op jit(solution)/shard_map/reduce_scatter | solution.py:195
  (915 shorter events, 693.9 us)
Async XLA Ops:
  6.5 1163.7 %reduce-scatter.2.cloned.1.call-start = ((), (), s32[]{:S(2)}) async-start(), calls=%async_computation.5 | async-start | bytes 2621440 | tf_op jit(solution)/shard_map/reduce_scatter | solution.py:195
  11.5 16.2 %all-to-all-start.2 = ((bf16[8,6,2048]{2,1,0:T(8,128)(2,1)}), bf16[8,6,2048]{2,1,0:T(8,128)(2,1)S(1)}, u32[]{:S(2)}, u32[]{:S(2)}) async-start(bf16[8,6,2048]{2,1,0:T(8,128)(2,1)} %reshape.369), calls=%async_computation.2 | async-start | bytes 524288 | tf_op jit(solution)/shard_map/while/body/eval_jaxpr/all_to_all | solution.py:132
  27.7 13.1 %all-to-all-start = ((bf16[8,6,2048]{2,1,0:T(8,128)(2,1)}), bf16[8,6,2048]{2,1,0:T(8,128)(2,1)S(1)}, u32[]{:S(2)}, u32[]{:S(2)}) async-start(bf16[8,6,2048]{2,1,0:T(8,128)(2,1)} %reshape.365), calls=%async_computation | async-start | bytes 524288 | tf_op jit(solution)/shard_map/while/body/eval_jaxpr/all_to_all | solution.py:131
  48.0 13.1 %all-to-all-start.3 = ((bf16[8,6,2048]{2,1,0:T(8,128)(2,1)}), bf16[8,6,2048]{2,1,0:T(8,128)(2,1)S(1)}, u32[]{:S(2)}, u32[]{:S(2)}) async-start(bf16[8,6,2048]{2,1,0:T(8,128)(2,1)} %reshape.371), calls=%async_computation.3 | async-start | bytes 524288 | tf_op jit(solution)/shard_map/while/body/eval_jaxpr/all_to_all | solution.py:148
  61.1 13.1 %all-to-all-start.1 = ((bf16[8,6,2048]{2,1,0:T(8,128)(2,1)}), bf16[8,6,2048]{2,1,0:T(8,128)(2,1)S(1)}, u32[]{:S(2)}, u32[]{:S(2)}) async-start(bf16[8,6,2048]{2,1,0:T(8,128)(2,1)} %reshape.367), calls=%async_computation.1 | async-start | bytes 524288 | tf_op jit(solution)/shard_map/while/body/eval_jaxpr/all_to_all | solution.py:147
  82.1 14.4 %all-to-all-start.2 = ((bf16[8,6,2048]{2,1,0:T(8,128)(2,1)}), bf16[8,6,2048]{2,1,0:T(8,128)(2,1)S(1)}, u32[]{:S(2)}, u32[]{:S(2)}) async-start(bf16[8,6,2048]{2,1,0:T(8,128)(2,1)} %reshape.369), calls=%async_computation.2 | async-start | bytes 524288 | tf_op jit(solution)/shard_map/while/body/eval_jaxpr/all_to_all | solution.py:132
  96.4 13.1 %all-to-all-start = ((bf16[8,6,2048]{2,1,0:T(8,128)(2,1)}), bf16[8,6,2048]{2,1,0:T(8,128)(2,1)S(1)}, u32[]{:S(2)}, u32[]{:S(2)}) async-start(bf16[8,6,2048]{2,1,0:T(8,128)(2,1)} %reshape.365), calls=%async_computation | async-start | bytes 524288 | tf_op jit(solution)/shard_map/while/body/eval_jaxpr/all_to_all | solution.py:131
  116.7 13.1 %all-to-all-start.3 = ((bf16[8,6,2048]{2,1,0:T(8,128)(2,1)}), bf16[8,6,2048]{2,1,0:T(8,128)(2,1)S(1)}, u32[]{:S(2)}, u32[]{:S(2)}) async-start(bf16[8,6,2048]{2,1,0:T(8,128)(2,1)} %reshape.371), calls=%async_computation.3 | async-start | bytes 524288 | tf_op jit(solution)/shard_map/while/body/eval_jaxpr/all_to_all | solution.py:148
  129.8 13.1 %all-to-all-start.1 = ((bf16[8,6,2048]{2,1,0:T(8,128)(2,1)}), bf16[8,6,2048]{2,1,0:T(8,128)(2,1)S(1)}, u32[]{:S(2)}, u32[]{:S(2)}) async-start(bf16[8,6,2048]{2,1,0:T(8,128)(2,1)} %reshape.367), calls=%async_computation.1 | async-start | bytes 524288 | tf_op jit(solution)/shard_map/while/body/eval_jaxpr/all_to_all | solution.py:147
  150.8 15.6 %all-to-all-start.2 = ((bf16[8,6,2048]{2,1,0:T(8,128)(2,1)}), bf16[8,6,2048]{2,1,0:T(8,128)(2,1)S(1)}, u32[]{:S(2)}, u32[]{:S(2)}) async-start(bf16[8,6,2048]{2,1,0:T(8,128)(2,1)} %reshape.369), calls=%async_computation.2 | async-start | bytes 524288 | tf_op jit(solution)/shard_map/while/body/eval_jaxpr/all_to_all | solution.py:132
  166.4 12.8 %all-to-all-start = ((bf16[8,6,2048]{2,1,0:T(8,128)(2,1)}), bf16[8,6,2048]{2,1,0:T(8,128)(2,1)S(1)}, u32[]{:S(2)}, u32[]{:S(2)}) async-start(bf16[8,6,2048]{2,1,0:T(8,128)(2,1)} %reshape.365), calls=%async_computation | async-start | bytes 524288 | tf_op jit(solution)/shard_map/while/body/eval_jaxpr/all_to_all | solution.py:131
  186.3 13.1 %all-to-all-start.3 = ((bf16[8,6,2048]{2,1,0:T(8,128)(2,1)}), bf16[8,6,2048]{2,1,0:T(8,128)(2,1)S(1)}, u32[]{:S(2)}, u32[]{:S(2)}) async-start(bf16[8,6,2048]{2,1,0:T(8,128)(2,1)} %reshape.371), calls=%async_computation.3 | async-start | bytes 524288 | tf_op jit(solution)/shard_map/while/body/eval_jaxpr/all_to_all | solution.py:148
  199.4 13.1 %all-to-all-start.1 = ((bf16[8,6,2048]{2,1,0:T(8,128)(2,1)}), bf16[8,6,2048]{2,1,0:T(8,128)(2,1)S(1)}, u32[]{:S(2)}, u32[]{:S(2)}) async-start(bf16[8,6,2048]{2,1,0:T(8,128)(2,1)} %reshape.367), calls=%async_computation.1 | async-start | bytes 524288 | tf_op jit(solution)/shard_map/while/body/eval_jaxpr/all_to_all | solution.py:147
  220.4 15.1 %all-to-all-start.2 = ((bf16[8,6,2048]{2,1,0:T(8,128)(2,1)}), bf16[8,6,2048]{2,1,0:T(8,128)(2,1)S(1)}, u32[]{:S(2)}, u32[]{:S(2)}) async-start(bf16[8,6,2048]{2,1,0:T(8,128)(2,1)} %reshape.369), calls=%async_computation.2 | async-start | bytes 524288 | tf_op jit(solution)/shard_map/while/body/eval_jaxpr/all_to_all | solution.py:132
  235.5 14.3 %all-to-all-start = ((bf16[8,6,2048]{2,1,0:T(8,128)(2,1)}), bf16[8,6,2048]{2,1,0:T(8,128)(2,1)S(1)}, u32[]{:S(2)}, u32[]{:S(2)}) async-start(bf16[8,6,2048]{2,1,0:T(8,128)(2,1)} %reshape.365), calls=%async_computation | async-start | bytes 524288 | tf_op jit(solution)/shard_map/while/body/eval_jaxpr/all_to_all | solution.py:131
  257.0 13.1 %all-to-all-start.3 = ((bf16[8,6,2048]{2,1,0:T(8,128)(2,1)}), bf16[8,6,2048]{2,1,0:T(8,128)(2,1)S(1)}, u32[]{:S(2)}, u32[]{:S(2)}) async-start(bf16[8,6,2048]{2,1,0:T(8,128)(2,1)} %reshape.371), calls=%async_computation.3 | async-start | bytes 524288 | tf_op jit(solution)/shard_map/while/body/eval_jaxpr/all_to_all | solution.py:148
  270.1 13.1 %all-to-all-start.1 = ((bf16[8,6,2048]{2,1,0:T(8,128)(2,1)}), bf16[8,6,2048]{2,1,0:T(8,128)(2,1)S(1)}, u32[]{:S(2)}, u32[]{:S(2)}) async-start(bf16[8,6,2048]{2,1,0:T(8,128)(2,1)} %reshape.367), calls=%async_computation.1 | async-start | bytes 524288 | tf_op jit(solution)/shard_map/while/body/eval_jaxpr/all_to_all | solution.py:147
  292.9 15.5 %all-to-all-start.2 = ((bf16[8,6,2048]{2,1,0:T(8,128)(2,1)}), bf16[8,6,2048]{2,1,0:T(8,128)(2,1)S(1)}, u32[]{:S(2)}, u32[]{:S(2)}) async-start(bf16[8,6,2048]{2,1,0:T(8,128)(2,1)} %reshape.369), calls=%async_computation.2 | async-start | bytes 524288 | tf_op jit(solution)/shard_map/while/body/eval_jaxpr/all_to_all | solution.py:132
  308.4 13.1 %all-to-all-start = ((bf16[8,6,2048]{2,1,0:T(8,128)(2,1)}), bf16[8,6,2048]{2,1,0:T(8,128)(2,1)S(1)}, u32[]{:S(2)}, u32[]{:S(2)}) async-start(bf16[8,6,2048]{2,1,0:T(8,128)(2,1)} %reshape.365), calls=%async_computation | async-start | bytes 524288 | tf_op jit(solution)/shard_map/while/body/eval_jaxpr/all_to_all | solution.py:131
  328.7 13.1 %all-to-all-start.3 = ((bf16[8,6,2048]{2,1,0:T(8,128)(2,1)}), bf16[8,6,2048]{2,1,0:T(8,128)(2,1)S(1)}, u32[]{:S(2)}, u32[]{:S(2)}) async-start(bf16[8,6,2048]{2,1,0:T(8,128)(2,1)} %reshape.371), calls=%async_computation.3 | async-start | bytes 524288 | tf_op jit(solution)/shard_map/while/body/eval_jaxpr/all_to_all | solution.py:148
  341.8 13.1 %all-to-all-start.1 = ((bf16[8,6,2048]{2,1,0:T(8,128)(2,1)}), bf16[8,6,2048]{2,1,0:T(8,128)(2,1)S(1)}, u32[]{:S(2)}, u32[]{:S(2)}) async-start(bf16[8,6,2048]{2,1,0:T(8,128)(2,1)} %reshape.367), calls=%async_computation.1 | async-start | bytes 524288 | tf_op jit(solution)/shard_map/while/body/eval_jaxpr/all_to_all | solution.py:147
  347.1 10.6 collective-permute-start.1
  367.7 15.5 %all-to-all-start.2 = ((bf16[8,6,2048]{2,1,0:T(8,128)(2,1)}), bf16[8,6,2048]{2,1,0:T(8,128)(2,1)S(1)}, u32[]{:S(2)}, u32[]{:S(2)}) async-start(bf16[8,6,2048]{2,1,0:T(8,128)(2,1)} %reshape.369), calls=%async_computation.2 | async-start | bytes 524288 | tf_op jit(solution)/shard_map/while/body/eval_jaxpr/all_to_all | solution.py:132
  383.2 13.1 %all-to-all-start = ((bf16[8,6,2048]{2,1,0:T(8,128)(2,1)}), bf16[8,6,2048]{2,1,0:T(8,128)(2,1)S(1)}, u32[]{:S(2)}, u32[]{:S(2)}) async-start(bf16[8,6,2048]{2,1,0:T(8,128)(2,1)} %reshape.365), calls=%async_computation | async-start | bytes 524288 | tf_op jit(solution)/shard_map/while/body/eval_jaxpr/all_to_all | solution.py:131
  403.4 13.1 %all-to-all-start.3 = ((bf16[8,6,2048]{2,1,0:T(8,128)(2,1)}), bf16[8,6,2048]{2,1,0:T(8,128)(2,1)S(1)}, u32[]{:S(2)}, u32[]{:S(2)}) async-start(bf16[8,6,2048]{2,1,0:T(8,128)(2,1)} %reshape.371), calls=%async_computation.3 | async-start | bytes 524288 | tf_op jit(solution)/shard_map/while/body/eval_jaxpr/all_to_all | solution.py:148
  416.5 13.1 %all-to-all-start.1 = ((bf16[8,6,2048]{2,1,0:T(8,128)(2,1)}), bf16[8,6,2048]{2,1,0:T(8,128)(2,1)S(1)}, u32[]{:S(2)}, u32[]{:S(2)}) async-start(bf16[8,6,2048]{2,1,0:T(8,128)(2,1)} %reshape.367), calls=%async_computation.1 | async-start | bytes 524288 | tf_op jit(solution)/shard_map/while/body/eval_jaxpr/all_to_all | solution.py:147
  421.9 10.6 collective-permute-start.1
  442.4 15.5 %all-to-all-start.2 = ((bf16[8,6,2048]{2,1,0:T(8,128)(2,1)}), bf16[8,6,2048]{2,1,0:T(8,128)(2,1)S(1)}, u32[]{:S(2)}, u32[]{:S(2)}) async-start(bf16[8,6,2048]{2,1,0:T(8,128)(2,1)} %reshape.369), calls=%async_computation.2 | async-start | bytes 524288 | tf_op jit(solution)/shard_map/while/body/eval_jaxpr/all_to_all | solution.py:132
  457.9 13.1 %all-to-all-start = ((bf16[8,6,2048]{2,1,0:T(8,128)(2,1)}), bf16[8,6,2048]{2,1,0:T(8,128)(2,1)S(1)}, u32[]{:S(2)}, u32[]{:S(2)}) async-start(bf16[8,6,2048]{2,1,0:T(8,128)(2,1)} %reshape.365), calls=%async_computation | async-start | bytes 524288 | tf_op jit(solution)/shard_map/while/body/eval_jaxpr/all_to_all | solution.py:131
  478.2 13.1 %all-to-all-start.3 = ((bf16[8,6,2048]{2,1,0:T(8,128)(2,1)}), bf16[8,6,2048]{2,1,0:T(8,128)(2,1)S(1)}, u32[]{:S(2)}, u32[]{:S(2)}) async-start(bf16[8,6,2048]{2,1,0:T(8,128)(2,1)} %reshape.371), calls=%async_computation.3 | async-start | bytes 524288 | tf_op jit(solution)/shard_map/while/body/eval_jaxpr/all_to_all | solution.py:148
  491.3 13.1 %all-to-all-start.1 = ((bf16[8,6,2048]{2,1,0:T(8,128)(2,1)}), bf16[8,6,2048]{2,1,0:T(8,128)(2,1)S(1)}, u32[]{:S(2)}, u32[]{:S(2)}) async-start(bf16[8,6,2048]{2,1,0:T(8,128)(2,1)} %reshape.367), calls=%async_computation.1 | async-start | bytes 524288 | tf_op jit(solution)/shard_map/while/body/eval_jaxpr/all_to_all | solution.py:147
  517.1 15.5 %all-to-all-start.2 = ((bf16[8,6,2048]{2,1,0:T(8,128)(2,1)}), bf16[8,6,2048]{2,1,0:T(8,128)(2,1)S(1)}, u32[]{:S(2)}, u32[]{:S(2)}) async-start(bf16[8,6,2048]{2,1,0:T(8,128)(2,1)} %reshape.369), calls=%async_computation.2 | async-start | bytes 524288 | tf_op jit(solution)/shard_map/while/body/eval_jaxpr/all_to_all | solution.py:132
  532.6 13.1 %all-to-all-start = ((bf16[8,6,2048]{2,1,0:T(8,128)(2,1)}), bf16[8,6,2048]{2,1,0:T(8,128)(2,1)S(1)}, u32[]{:S(2)}, u32[]{:S(2)}) async-start(bf16[8,6,2048]{2,1,0:T(8,128)(2,1)} %reshape.365), calls=%async_computation | async-start | bytes 524288 | tf_op jit(solution)/shard_map/while/body/eval_jaxpr/all_to_all | solution.py:131
  552.9 13.1 %all-to-all-start.3 = ((bf16[8,6,2048]{2,1,0:T(8,128)(2,1)}), bf16[8,6,2048]{2,1,0:T(8,128)(2,1)S(1)}, u32[]{:S(2)}, u32[]{:S(2)}) async-start(bf16[8,6,2048]{2,1,0:T(8,128)(2,1)} %reshape.371), calls=%async_computation.3 | async-start | bytes 524288 | tf_op jit(solution)/shard_map/while/body/eval_jaxpr/all_to_all | solution.py:148
  566.0 13.1 %all-to-all-start.1 = ((bf16[8,6,2048]{2,1,0:T(8,128)(2,1)}), bf16[8,6,2048]{2,1,0:T(8,128)(2,1)S(1)}, u32[]{:S(2)}, u32[]{:S(2)}) async-start(bf16[8,6,2048]{2,1,0:T(8,128)(2,1)} %reshape.367), calls=%async_computation.1 | async-start | bytes 524288 | tf_op jit(solution)/shard_map/while/body/eval_jaxpr/all_to_all | solution.py:147
  591.9 15.5 %all-to-all-start.2 = ((bf16[8,6,2048]{2,1,0:T(8,128)(2,1)}), bf16[8,6,2048]{2,1,0:T(8,128)(2,1)S(1)}, u32[]{:S(2)}, u32[]{:S(2)}) async-start(bf16[8,6,2048]{2,1,0:T(8,128)(2,1)} %reshape.369), calls=%async_computation.2 | async-start | bytes 524288 | tf_op jit(solution)/shard_map/while/body/eval_jaxpr/all_to_all | solution.py:132
  607.4 13.1 %all-to-all-start = ((bf16[8,6,2048]{2,1,0:T(8,128)(2,1)}), bf16[8,6,2048]{2,1,0:T(8,128)(2,1)S(1)}, u32[]{:S(2)}, u32[]{:S(2)}) async-start(bf16[8,6,2048]{2,1,0:T(8,128)(2,1)} %reshape.365), calls=%async_computation | async-start | bytes 524288 | tf_op jit(solution)/shard_map/while/body/eval_jaxpr/all_to_all | solution.py:131
  627.6 13.1 %all-to-all-start.3 = ((bf16[8,6,2048]{2,1,0:T(8,128)(2,1)}), bf16[8,6,2048]{2,1,0:T(8,128)(2,1)S(1)}, u32[]{:S(2)}, u32[]{:S(2)}) async-start(bf16[8,6,2048]{2,1,0:T(8,128)(2,1)} %reshape.371), calls=%async_computation.3 | async-start | bytes 524288 | tf_op jit(solution)/shard_map/while/body/eval_jaxpr/all_to_all | solution.py:148
  640.7 13.1 %all-to-all-start.1 = ((bf16[8,6,2048]{2,1,0:T(8,128)(2,1)}), bf16[8,6,2048]{2,1,0:T(8,128)(2,1)S(1)}, u32[]{:S(2)}, u32[]{:S(2)}) async-start(bf16[8,6,2048]{2,1,0:T(8,128)(2,1)} %reshape.367), calls=%async_computation.1 | async-start | bytes 524288 | tf_op jit(solution)/shard_map/while/body/eval_jaxpr/all_to_all | solution.py:147
  666.6 15.5 %all-to-all-start.2 = ((bf16[8,6,2048]{2,1,0:T(8,128)(2,1)}), bf16[8,6,2048]{2,1,0:T(8,128)(2,1)S(1)}, u32[]{:S(2)}, u32[]{:S(2)}) async-start(bf16[8,6,2048]{2,1,0:T(8,128)(2,1)} %reshape.369), calls=%async_computation.2 | async-start | bytes 524288 | tf_op jit(solution)/shard_map/while/body/eval_jaxpr/all_to_all | solution.py:132
  682.1 13.1 %all-to-all-start = ((bf16[8,6,2048]{2,1,0:T(8,128)(2,1)}), bf16[8,6,2048]{2,1,0:T(8,128)(2,1)S(1)}, u32[]{:S(2)}, u32[]{:S(2)}) async-start(bf16[8,6,2048]{2,1,0:T(8,128)(2,1)} %reshape.365), calls=%async_computation | async-start | bytes 524288 | tf_op jit(solution)/shard_map/while/body/eval_jaxpr/all_to_all | solution.py:131
  702.4 13.1 %all-to-all-start.3 = ((bf16[8,6,2048]{2,1,0:T(8,128)(2,1)}), bf16[8,6,2048]{2,1,0:T(8,128)(2,1)S(1)}, u32[]{:S(2)}, u32[]{:S(2)}) async-start(bf16[8,6,2048]{2,1,0:T(8,128)(2,1)} %reshape.371), calls=%async_computation.3 | async-start | bytes 524288 | tf_op jit(solution)/shard_map/while/body/eval_jaxpr/all_to_all | solution.py:148
  715.5 13.1 %all-to-all-start.1 = ((bf16[8,6,2048]{2,1,0:T(8,128)(2,1)}), bf16[8,6,2048]{2,1,0:T(8,128)(2,1)S(1)}, u32[]{:S(2)}, u32[]{:S(2)}) async-start(bf16[8,6,2048]{2,1,0:T(8,128)(2,1)} %reshape.367), calls=%async_computation.1 | async-start | bytes 524288 | tf_op jit(solution)/shard_map/while/body/eval_jaxpr/all_to_all | solution.py:147
  741.4 15.5 %all-to-all-start.2 = ((bf16[8,6,2048]{2,1,0:T(8,128)(2,1)}), bf16[8,6,2048]{2,1,0:T(8,128)(2,1)S(1)}, u32[]{:S(2)}, u32[]{:S(2)}) async-start(bf16[8,6,2048]{2,1,0:T(8,128)(2,1)} %reshape.369), calls=%async_computation.2 | async-start | bytes 524288 | tf_op jit(solution)/shard_map/while/body/eval_jaxpr/all_to_all | solution.py:132
  756.8 13.1 %all-to-all-start = ((bf16[8,6,2048]{2,1,0:T(8,128)(2,1)}), bf16[8,6,2048]{2,1,0:T(8,128)(2,1)S(1)}, u32[]{:S(2)}, u32[]{:S(2)}) async-start(bf16[8,6,2048]{2,1,0:T(8,128)(2,1)} %reshape.365), calls=%async_computation | async-start | bytes 524288 | tf_op jit(solution)/shard_map/while/body/eval_jaxpr/all_to_all | solution.py:131
  777.1 13.1 %all-to-all-start.3 = ((bf16[8,6,2048]{2,1,0:T(8,128)(2,1)}), bf16[8,6,2048]{2,1,0:T(8,128)(2,1)S(1)}, u32[]{:S(2)}, u32[]{:S(2)}) async-start(bf16[8,6,2048]{2,1,0:T(8,128)(2,1)} %reshape.371), calls=%async_computation.3 | async-start | bytes 524288 | tf_op jit(solution)/shard_map/while/body/eval_jaxpr/all_to_all | solution.py:148
  790.2 13.1 %all-to-all-start.1 = ((bf16[8,6,2048]{2,1,0:T(8,128)(2,1)}), bf16[8,6,2048]{2,1,0:T(8,128)(2,1)S(1)}, u32[]{:S(2)}, u32[]{:S(2)}) async-start(bf16[8,6,2048]{2,1,0:T(8,128)(2,1)} %reshape.367), calls=%async_computation.1 | async-start | bytes 524288 | tf_op jit(solution)/shard_map/while/body/eval_jaxpr/all_to_all | solution.py:147
  816.1 15.5 %all-to-all-start.2 = ((bf16[8,6,2048]{2,1,0:T(8,128)(2,1)}), bf16[8,6,2048]{2,1,0:T(8,128)(2,1)S(1)}, u32[]{:S(2)}, u32[]{:S(2)}) async-start(bf16[8,6,2048]{2,1,0:T(8,128)(2,1)} %reshape.369), calls=%async_computation.2 | async-start | bytes 524288 | tf_op jit(solution)/shard_map/while/body/eval_jaxpr/all_to_all | solution.py:132
  831.6 13.1 %all-to-all-start = ((bf16[8,6,2048]{2,1,0:T(8,128)(2,1)}), bf16[8,6,2048]{2,1,0:T(8,128)(2,1)S(1)}, u32[]{:S(2)}, u32[]{:S(2)}) async-start(bf16[8,6,2048]{2,1,0:T(8,128)(2,1)} %reshape.365), calls=%async_computation | async-start | bytes 524288 | tf_op jit(solution)/shard_map/while/body/eval_jaxpr/all_to_all | solution.py:131
  851.9 13.1 %all-to-all-start.3 = ((bf16[8,6,2048]{2,1,0:T(8,128)(2,1)}), bf16[8,6,2048]{2,1,0:T(8,128)(2,1)S(1)}, u32[]{:S(2)}, u32[]{:S(2)}) async-start(bf16[8,6,2048]{2,1,0:T(8,128)(2,1)} %reshape.371), calls=%async_computation.3 | async-start | bytes 524288 | tf_op jit(solution)/shard_map/while/body/eval_jaxpr/all_to_all | solution.py:148
  864.9 13.1 %all-to-all-start.1 = ((bf16[8,6,2048]{2,1,0:T(8,128)(2,1)}), bf16[8,6,2048]{2,1,0:T(8,128)(2,1)S(1)}, u32[]{:S(2)}, u32[]{:S(2)}) async-start(bf16[8,6,2048]{2,1,0:T(8,128)(2,1)} %reshape.367), calls=%async_computation.1 | async-start | bytes 524288 | tf_op jit(solution)/shard_map/while/body/eval_jaxpr/all_to_all | solution.py:147
  890.8 15.5 %all-to-all-start.2 = ((bf16[8,6,2048]{2,1,0:T(8,128)(2,1)}), bf16[8,6,2048]{2,1,0:T(8,128)(2,1)S(1)}, u32[]{:S(2)}, u32[]{:S(2)}) async-start(bf16[8,6,2048]{2,1,0:T(8,128)(2,1)} %reshape.369), calls=%async_computation.2 | async-start | bytes 524288 | tf_op jit(solution)/shard_map/while/body/eval_jaxpr/all_to_all | solution.py:132
  906.3 13.1 %all-to-all-start = ((bf16[8,6,2048]{2,1,0:T(8,128)(2,1)}), bf16[8,6,2048]{2,1,0:T(8,128)(2,1)S(1)}, u32[]{:S(2)}, u32[]{:S(2)}) async-start(bf16[8,6,2048]{2,1,0:T(8,128)(2,1)} %reshape.365), calls=%async_computation | async-start | bytes 524288 | tf_op jit(solution)/shard_map/while/body/eval_jaxpr/all_to_all | solution.py:131
  926.6 13.1 %all-to-all-start.3 = ((bf16[8,6,2048]{2,1,0:T(8,128)(2,1)}), bf16[8,6,2048]{2,1,0:T(8,128)(2,1)S(1)}, u32[]{:S(2)}, u32[]{:S(2)}) async-start(bf16[8,6,2048]{2,1,0:T(8,128)(2,1)} %reshape.371), calls=%async_computation.3 | async-start | bytes 524288 | tf_op jit(solution)/shard_map/while/body/eval_jaxpr/all_to_all | solution.py:148
  939.7 13.1 %all-to-all-start.1 = ((bf16[8,6,2048]{2,1,0:T(8,128)(2,1)}), bf16[8,6,2048]{2,1,0:T(8,128)(2,1)S(1)}, u32[]{:S(2)}, u32[]{:S(2)}) async-start(bf16[8,6,2048]{2,1,0:T(8,128)(2,1)} %reshape.367), calls=%async_computation.1 | async-start | bytes 524288 | tf_op jit(solution)/shard_map/while/body/eval_jaxpr/all_to_all | solution.py:147
  945.0 10.6 collective-permute-start.1
  965.6 15.5 %all-to-all-start.2 = ((bf16[8,6,2048]{2,1,0:T(8,128)(2,1)}), bf16[8,6,2048]{2,1,0:T(8,128)(2,1)S(1)}, u32[]{:S(2)}, u32[]{:S(2)}) async-start(bf16[8,6,2048]{2,1,0:T(8,128)(2,1)} %reshape.369), calls=%async_computation.2 | async-start | bytes 524288 | tf_op jit(solution)/shard_map/while/body/eval_jaxpr/all_to_all | solution.py:132
  981.0 13.1 %all-to-all-start = ((bf16[8,6,2048]{2,1,0:T(8,128)(2,1)}), bf16[8,6,2048]{2,1,0:T(8,128)(2,1)S(1)}, u32[]{:S(2)}, u32[]{:S(2)}) async-start(bf16[8,6,2048]{2,1,0:T(8,128)(2,1)} %reshape.365), calls=%async_computation | async-start | bytes 524288 | tf_op jit(solution)/shard_map/while/body/eval_jaxpr/all_to_all | solution.py:131
  1001.3 13.1 %all-to-all-start.3 = ((bf16[8,6,2048]{2,1,0:T(8,128)(2,1)}), bf16[8,6,2048]{2,1,0:T(8,128)(2,1)S(1)}, u32[]{:S(2)}, u32[]{:S(2)}) async-start(bf16[8,6,2048]{2,1,0:T(8,128)(2,1)} %reshape.371), calls=%async_computation.3 | async-start | bytes 524288 | tf_op jit(solution)/shard_map/while/body/eval_jaxpr/all_to_all | solution.py:148
  1014.4 13.1 %all-to-all-start.1 = ((bf16[8,6,2048]{2,1,0:T(8,128)(2,1)}), bf16[8,6,2048]{2,1,0:T(8,128)(2,1)S(1)}, u32[]{:S(2)}, u32[]{:S(2)}) async-start(bf16[8,6,2048]{2,1,0:T(8,128)(2,1)} %reshape.367), calls=%async_computation.1 | async-start | bytes 524288 | tf_op jit(solution)/shard_map/while/body/eval_jaxpr/all_to_all | solution.py:147
  1040.3 15.5 %all-to-all-start.2 = ((bf16[8,6,2048]{2,1,0:T(8,128)(2,1)}), bf16[8,6,2048]{2,1,0:T(8,128)(2,1)S(1)}, u32[]{:S(2)}, u32[]{:S(2)}) async-start(bf16[8,6,2048]{2,1,0:T(8,128)(2,1)} %reshape.369), calls=%async_computation.2 | async-start | bytes 524288 | tf_op jit(solution)/shard_map/while/body/eval_jaxpr/all_to_all | solution.py:132
  1055.8 13.1 %all-to-all-start = ((bf16[8,6,2048]{2,1,0:T(8,128)(2,1)}), bf16[8,6,2048]{2,1,0:T(8,128)(2,1)S(1)}, u32[]{:S(2)}, u32[]{:S(2)}) async-start(bf16[8,6,2048]{2,1,0:T(8,128)(2,1)} %reshape.365), calls=%async_computation | async-start | bytes 524288 | tf_op jit(solution)/shard_map/while/body/eval_jaxpr/all_to_all | solution.py:131
  1076.1 13.1 %all-to-all-start.3 = ((bf16[8,6,2048]{2,1,0:T(8,128)(2,1)}), bf16[8,6,2048]{2,1,0:T(8,128)(2,1)S(1)}, u32[]{:S(2)}, u32[]{:S(2)}) async-start(bf16[8,6,2048]{2,1,0:T(8,128)(2,1)} %reshape.371), calls=%async_computation.3 | async-start | bytes 524288 | tf_op jit(solution)/shard_map/while/body/eval_jaxpr/all_to_all | solution.py:148
  1089.2 13.1 %all-to-all-start.1 = ((bf16[8,6,2048]{2,1,0:T(8,128)(2,1)}), bf16[8,6,2048]{2,1,0:T(8,128)(2,1)S(1)}, u32[]{:S(2)}, u32[]{:S(2)}) async-start(bf16[8,6,2048]{2,1,0:T(8,128)(2,1)} %reshape.367), calls=%async_computation.1 | async-start | bytes 524288 | tf_op jit(solution)/shard_map/while/body/eval_jaxpr/all_to_all | solution.py:147
  (104 other events, 794.9 us)
Sparse Core Ops, SparseCore 0:
  1119.9 50.3 reduce-scatter.1
where the time goes:
time: 1190 us; the launch traced here: 1180 us
  waiting for transfers between devices  522 us (44%)
  starting transfers between devices  319 us (27%)
  matrix products  175 us (15%)
  local copies, waits for them, and re-layouts  102 us (9%)
  other arithmetic  45.2 us (4%)
  between operations  13.4 us (1%)
    dot_general x90, matrix products, contract_last(): lax.dot_general(left, right, (((1,), (1,)), ((), ())), preferred_element_...  120 us
    all_to_all x15, waiting for transfers between devices, advance(): lax.all_to_all(send_adjoint, 'expert', split_axis=0, concat_axis=0, tiled...  117 us
    ppermute x30, waiting for transfers between devices, passed_along(): lax.ppermute(value, axis, [(source, source + steps) for source in range(f...  101 us
    all_to_all x15, waiting for transfers between devices, advance(): lax.all_to_all(back_adjoint, 'expert', split_axis=0, concat_axis=0, tiled...  96.5 us
    all_to_all x15, waiting for transfers between devices, advance(): lax.all_to_all(send_tangent, 'expert', split_axis=0, concat_axis=0, tiled...  87.5 us
    all_to_all x15, starting transfers between devices, advance(): lax.all_to_all(send_tangent, 'expert', split_axis=0, concat_axis=0, tiled...  83.3 us
    all_to_all x15, waiting for transfers between devices, advance(): lax.all_to_all(back_tangent, 'expert', split_axis=0, concat_axis=0, tiled...  69.3 us
    all_to_all x15, starting transfers between devices, advance(): lax.all_to_all(send_adjoint, 'expert', split_axis=0, concat_axis=0, tiled...  66.2 us
  transfers between devices with their start and end apart: 91, of which 87 were waited for; matrix products, arithmetic and copies ran while one was open for 14% of the time, Pallas kernels for 0%

commit v1 on v0

v1 whole, which is shorter than its diff:
```python
import functools

import jax
import jax.numpy as jnp
import numpy as np
from jax import lax
from jax.experimental import pallas as pl
from jax.experimental.pallas import tpu as pltpu
from jax.sharding import PartitionSpec as P

M = 8
T_MB = 16
TOP = 2
QUARTERS = 4
CHUNKS = 2
KINDS = 2
MESH = pl.DeviceIdType.MESH
F32 = jnp.float32
BF16 = jnp.bfloat16


def dot(left, right, dims):
    return lax.dot_general(left, right, (dims, ((), ())), preferred_element_type=F32)


def wait_bytes(view, sem):
    pltpu.make_async_copy(view, view, sem).wait()


def relay_kernel(
    sizes,
    target_ref,
    weight_ref,
    order_ref,
    unorder_ref,
    adjoint_ref,
    saved_ref,
    gate_ref,
    up_ref,
    down_ref,
    probe_ref,
    out_ref,
    target_above,
    token_in,
    token_now,
    pick_send,
    pick_recv,
    back_send,
    back_recv,
    pick_rows,
    block_rows,
    hidden_rows,
    factors,
    grads,
    total,
    table_send_sem,
    table_recv_sem,
    token_send_sem,
    token_recv_sem,
    pick_send_sem,
    pick_recv_sem,
    back_send_sem,
    back_recv_sem,
    block_send_sem,
    block_recv_sem,
    hidden_send_sem,
    hidden_recv_sem,
):
    stages, experts, replicas, capacity = sizes
    stage = lax.axis_index("pipe")
    expert = lax.axis_index("expert")
    replica = lax.axis_index("dp")
    below = lax.rem(stage + stages - 1, stages)
    above = lax.rem(stage + 1, stages)
    is_top = stage == stages - 1
    is_bottom = stage == 0
    slots = experts * capacity
    wire = QUARTERS * KINDS * capacity
    lanes = pick_send.shape[-1]
    quarter = lanes * CHUNKS
    width = gate_ref.shape[1]
    pair = KINDS * slots
    block = QUARTERS // replicas

    barrier = pltpu.get_barrier_semaphore()

    def greet(peer, carry):
        pl.semaphore_signal(
            barrier, inc=1, device_id={"pipe": below, "expert": peer}, device_id_type=MESH
        )
        pl.semaphore_signal(
            barrier, inc=1, device_id={"pipe": above, "expert": peer}, device_id_type=MESH
        )
        return carry

    lax.fori_loop(0, experts, greet, 0)
    for step in range(1, experts):
        pl.semaphore_signal(
            barrier,
            inc=1,
            device_id={"expert": lax.rem(expert + step, experts)},
            device_id_type=MESH,
        )
    for step in range(1, replicas):
        pl.semaphore_signal(
            barrier,
            inc=1,
            device_id={"dp": lax.rem(replica + step, replicas)},
            device_id_type=MESH,
        )
    pl.semaphore_wait(barrier, 2 * experts + experts - 1 + replicas - 1)

    table_copy = pltpu.make_async_remote_copy(
        src_ref=target_ref,
        dst_ref=target_above,
        send_sem=table_send_sem,
        recv_sem=table_recv_sem,
        device_id={"pipe": below},
        device_id_type=MESH,
    )

    @pl.when(jnp.logical_not(is_bottom))
    def _():
        table_copy.start()

    @pl.when(jnp.logical_not(is_top))
    def _():
        table_copy.wait_recv()

    rows = lax.broadcasted_iota(jnp.int32, (experts * wire, 128), 0)

    def matches(table, micro):
        pair_rows = table[micro]
        return rows == pair_rows[0:1, :], rows == pair_rows[1:2, :]

    def curvature(micro):
        wait_bytes(block_rows.at[micro], block_recv_sem.at[micro])
        wait_bytes(hidden_rows.at[micro, pl.ds(0, replicas - 1)], hidden_recv_sem.at[micro])
        right = hidden_rows[micro].reshape(replicas * pair, width)
        for chunk in range(CHUNKS):
            for part in range(block):
                left = block_rows[micro, chunk, :, part * pair : (part + 1) * pair, :]
                found = dot(left.reshape(replicas * pair, lanes), right, ((0,), (0,)))
                start = part * quarter + chunk * lanes
                here = slice(start, start + lanes)

                @pl.when(micro == 0)
                def _():
                    total[here, :] = found

                @pl.when(micro > 0)
                def _():
                    total[here, :] = total[here, :] + found

    def advance(micro, carry):
        first, second = matches(target_ref, micro)
        weights = weight_ref[micro]
        placing = jnp.where(first | second, 1.0, 0.0).astype(BF16)
        scale = jnp.sum(
            jnp.where(first, weights[0:1, :], 0.0) + jnp.where(second, weights[1:2, :], 0.0),
            axis=1,
            keepdims=True,
        )

        for chunk in range(CHUNKS):

            @pl.when(is_top)
            def _():
                row_start = pl.multiple_of(micro * T_MB, T_MB)
                for part in range(QUARTERS):
                    start = part * quarter + chunk * lanes
                    base = part * KINDS * T_MB
                    token_now[micro, chunk, base : base + T_MB, :] = adjoint_ref[
                        pl.ds(row_start, T_MB), start : start + lanes
                    ]
                    token_now[micro, chunk, base + T_MB : base + 2 * T_MB, :] = jnp.zeros(
                        (T_MB, lanes), BF16
                    )

            @pl.when(jnp.logical_not(is_top))
            def _():
                above_first, above_second = matches(target_above, micro)
                merging = jnp.where(above_first | above_second, 1.0, 0.0).astype(BF16)
                wait_bytes(token_in.at[micro, chunk], token_recv_sem.at[micro, chunk])
                wait_bytes(back_recv.at[micro, chunk], back_recv_sem.at[micro, chunk])
                returned = back_recv[micro, chunk].reshape(experts * wire, lanes)
                token_now[micro, chunk] = (
                    token_in[micro, chunk].astype(F32) + dot(merging, returned, ((0,), (0,)))
                ).astype(BF16)

            picked = dot(placing, token_now[micro, chunk], ((1,), (0,))) * scale
            pick_send[micro, chunk] = picked.astype(BF16).reshape(experts, wire, lanes)
            for step in range(1, experts):
                peer = lax.rem(expert + step, experts)
                pltpu.make_async_remote_copy(
                    src_ref=pick_send.at[micro, chunk, peer],
                    dst_ref=pick_recv.at[micro, chunk, expert],
                    send_sem=pick_send_sem.at[micro],
                    recv_sem=pick_recv_sem.at[micro, chunk],
                    device_id={"expert": peer},
                    device_id_type=MESH,
                ).start()
            pltpu.make_async_copy(
                pick_send.at[micro, chunk, expert],
                pick_recv.at[micro, chunk, expert],
                pick_recv_sem.at[micro, chunk],
            ).start()

            @pl.when(jnp.logical_not(is_bottom))
            def _():
                pltpu.make_async_remote_copy(
                    src_ref=token_now.at[micro, chunk],
                    dst_ref=token_in.at[micro, chunk],
                    send_sem=token_send_sem.at[micro],
                    recv_sem=token_recv_sem.at[micro, chunk],
                    device_id={"pipe": below},
                    device_id_type=MESH,
                ).start()

        pre_gate = saved_ref[micro, 0].astype(F32)
        pre_up = saved_ref[micro, 1].astype(F32)
        tangent_gate = saved_ref[micro, 2].astype(F32)
        tangent_up = saved_ref[micro, 3].astype(F32)
        sigmoid = jax.nn.sigmoid(pre_gate)
        silu = pre_gate * sigmoid
        slope = sigmoid * (1.0 + pre_gate * (1.0 - sigmoid))
        bend = sigmoid * (1.0 - sigmoid) * (2.0 + pre_gate * (1.0 - 2.0 * sigmoid))
        hidden_rows[micro, replica, 0:slots, :] = (
            slope * tangent_gate * pre_up + silu * tangent_up
        ).astype(BF16)
        hidden_rows[micro, replica, slots:pair, :] = (silu * pre_up).astype(BF16)
        for step in range(1, replicas):
            pltpu.make_async_remote_copy(
                src_ref=hidden_rows.at[micro, replica],
                dst_ref=hidden_rows.at[micro, replica],
                send_sem=hidden_send_sem.at[micro],
                recv_sem=hidden_recv_sem.at[micro],
                device_id={"dp": lax.rem(replica + step, replicas)},
                device_id_type=MESH,
            ).start()
        factors[0] = pre_up * slope
        factors[1] = silu
        factors[2] = tangent_up * slope + pre_up * bend * tangent_gate
        factors[3] = slope * tangent_gate

        @pl.when(micro > 0)
        def _():
            curvature(micro - 1)

        for chunk in range(CHUNKS):
            wait_bytes(pick_recv.at[micro, chunk], pick_recv_sem.at[micro, chunk])
            received = pick_recv[micro, chunk].reshape(experts * wire, lanes)
            ordered = dot(order_ref[...], received, ((1,), (0,))).astype(BF16)
            pick_rows[micro, chunk] = ordered
            for step in range(1, replicas):
                peer = lax.rem(replica + step, replicas)
                pltpu.make_async_remote_copy(
                    src_ref=pick_rows.at[micro, chunk, pl.ds(peer * (block * pair), block * pair)],
                    dst_ref=block_rows.at[micro, chunk, replica],
                    send_sem=block_send_sem.at[micro],
                    recv_sem=block_recv_sem.at[micro],
                    device_id={"dp": peer},
                    device_id_type=MESH,
                ).start()
            pltpu.make_async_copy(
                pick_rows.at[micro, chunk, pl.ds(replica * (block * pair), block * pair)],
                block_rows.at[micro, chunk, replica],
                block_recv_sem.at[micro],
            ).start()

            @pl.when(jnp.logical_not(is_bottom))
            def _():
                both = jnp.concatenate(
                    [ordered[part * pair : (part + 1) * pair, :] for part in range(QUARTERS)],
                    axis=1,
                )
                starts = [part * quarter + chunk * lanes for part in range(QUARTERS)]
                down = jnp.concatenate(
                    [down_ref[:, start : start + lanes] for start in starts], axis=1
                )
                aside = jnp.concatenate(
                    [probe_ref[start : start + lanes, :] for start in starts], axis=0
                )
                main = dot(both, down, ((1,), (1,)))
                extra = dot(both[0:slots, :], aside, ((1,), (0,)))
                if chunk == 0:
                    grads[0] = main[0:slots, :]
                    grads[1] = main[slots:pair, :] + extra
                else:
                    grads[0] = grads[0] + main[0:slots, :]
                    grads[1] = grads[1] + (main[slots:pair, :] + extra)

        @pl.when(jnp.logical_not(is_bottom))
        def _():
            grad = grads[0]
            grad_dot = grads[1]
            left = jnp.concatenate(
                [
                    jnp.concatenate(
                        [
                            (grad * factors[0]).astype(BF16),
                            (grad_dot * factors[0] + grad * factors[2]).astype(BF16),
                        ],
                        axis=0,
                    ),
                    jnp.concatenate(
                        [
                            (grad * factors[1]).astype(BF16),
                            (grad_dot * factors[1] + grad * factors[3]).astype(BF16),
                        ],
                        axis=0,
                    ),
                ],
                axis=1,
            )
            for chunk in range(CHUNKS):
                starts = [part * quarter + chunk * lanes for part in range(QUARTERS)]
                right = jnp.concatenate(
                    [
                        jnp.concatenate(
                            [gate_ref[start : start + lanes, :] for start in starts], axis=0
                        ),
                        jnp.concatenate(
                            [up_ref[start : start + lanes, :] for start in starts], axis=0
                        ),
                    ],
                    axis=1,
                )
                back = dot(left, right, ((1,), (1,))).astype(BF16)
                stacked = jnp.concatenate(
                    [back[:, part * lanes : (part + 1) * lanes] for part in range(QUARTERS)],
                    axis=0,
                )
                back_send[micro, chunk] = (
                    dot(unorder_ref[...], stacked, ((1,), (0,)))
                    .astype(BF16)
                    .reshape(experts, wire, lanes)
                )
                for step in range(experts):
                    peer = lax.rem(expert + step, experts)
                    pltpu.make_async_remote_copy(
                        src_ref=back_send.at[micro, chunk, peer],
                        dst_ref=back_recv.at[micro, chunk, expert],
                        send_sem=back_send_sem.at[micro],
                        recv_sem=back_recv_sem.at[micro, chunk],
                        device_id={"pipe": below, "expert": peer},
                        device_id_type=MESH,
                    ).start()

        return carry

    lax.fori_loop(0, M, advance, 0)
    curvature(M - 1)
    rows_here = block * quarter
    start = pl.multiple_of(replica * rows_here, rows_here)
    out_ref[...] = probe_ref[pl.ds(start, rows_here), :].astype(F32) * total[...]

    def settle(micro, carry):
        wait_bytes(pick_send.at[micro, :, pl.ds(0, experts - 1)], pick_send_sem.at[micro])
        wait_bytes(hidden_rows.at[micro, pl.ds(0, replicas - 1)], hidden_send_sem.at[micro])
        wait_bytes(
            block_rows.at[micro, :, pl.ds(0, replicas - 1)], block_send_sem.at[micro]
        )

        @pl.when(jnp.logical_not(is_bottom))
        def _():
            wait_bytes(back_send.at[micro], back_send_sem.at[micro])
            wait_bytes(token_now.at[micro], token_send_sem.at[micro])

        return carry

    lax.fori_loop(0, M, settle, 0)

    @pl.when(jnp.logical_not(is_bottom))
    def _():
        table_copy.wait_send()


def row_orders(experts, capacity):
    slots = experts * capacity
    count = QUARTERS * KINDS * slots
    order = np.zeros((count, count), np.float32)
    for kind in range(QUARTERS * KINDS):
        for source in range(experts):
            for slot in range(capacity):
                order[
                    kind * slots + source * capacity + slot,
                    (source * QUARTERS * KINDS + kind) * capacity + slot,
                ] = 1.0
    return order


def pick_tables(routes, probs, capacity):
    picks = T_MB * TOP
    flat = routes.reshape(M, picks)
    index = jnp.arange(picks, dtype=jnp.int32)
    earlier = index[None, :] < index[:, None]
    same = flat[:, :, None] == flat[:, None, :]
    position = jnp.sum((same & earlier[None]).astype(jnp.int32), axis=2)
    parts = QUARTERS * KINDS
    base = (flat * (parts * capacity) + position).reshape(M, T_MB, TOP).transpose(0, 2, 1)
    offset = jnp.arange(parts, dtype=jnp.int32) * capacity
    target = (base[:, :, None, :] + offset[None, None, :, None]).reshape(M, TOP, parts * T_MB)
    weight = jnp.broadcast_to(
        probs.reshape(M, T_MB, TOP).transpose(0, 2, 1)[:, :, None, :], (M, TOP, parts, T_MB)
    ).reshape(M, TOP, parts * T_MB)
    return target, weight


def per_device(adjoint_out, gate_probs, routes, saved, w_gate, w_up, w_down, probe):
    stages = lax.axis_size("pipe")
    experts = lax.axis_size("expert")
    replicas = lax.axis_size("dp")
    slots = saved.shape[5]
    capacity = slots // experts
    model = adjoint_out.shape[1]
    width = w_gate.shape[3]
    lanes = model // QUARTERS // CHUNKS
    wire = QUARTERS * KINDS * capacity
    tokens = QUARTERS * KINDS * T_MB
    pair = KINDS * slots
    block = QUARTERS // replicas
    target, weight = pick_tables(routes[0], gate_probs[0], capacity)
    order = row_orders(experts, capacity)
    vmem = pl.BlockSpec(memory_space=pltpu.VMEM)
    dma = pltpu.SemaphoreType.DMA
    found = pl.pallas_call(
        functools.partial(relay_kernel, (stages, experts, replicas, capacity)),
        out_shape=jax.ShapeDtypeStruct((model // replicas, width), F32),
        in_specs=[vmem] * 10,
        out_specs=vmem,
        scratch_shapes=[
            pltpu.VMEM((M, TOP, tokens), jnp.int32),
            pltpu.VMEM((M, CHUNKS, tokens, lanes), BF16),
            pltpu.VMEM((M, CHUNKS, tokens, lanes), BF16),
            pltpu.VMEM((M, CHUNKS, experts, wire, lanes), BF16),
            pltpu.VMEM((M, CHUNKS, experts, wire, lanes), BF16),
            pltpu.VMEM((M, CHUNKS, experts, wire, lanes), BF16),
            pltpu.VMEM((M, CHUNKS, experts, wire, lanes), BF16),
            pltpu.VMEM((M, CHUNKS, QUARTERS * pair, lanes), BF16),
            pltpu.VMEM((M, CHUNKS, replicas, block * pair, lanes), BF16),
            pltpu.VMEM((M, replicas, pair, width), BF16),
            pltpu.VMEM((4, slots, width), F32),
            pltpu.VMEM((2, slots, width), F32),
            pltpu.VMEM((model // replicas, width), F32),
            dma,
            dma,
            dma((M,)),
            dma((M, CHUNKS)),
            dma((M,)),
            dma((M, CHUNKS)),
            dma((M,)),
            dma((M, CHUNKS)),
            dma((M,)),
            dma((M,)),
            dma((M,)),
            dma((M,)),
        ],
        compiler_params=pltpu.CompilerParams(
            collective_id=0, has_side_effects=True, vmem_limit_bytes=60 * 1024 * 1024
        ),
        name="relay",
    )(
        target,
        weight,
        jnp.asarray(order, BF16),
        jnp.asarray(order.T, BF16),
        adjoint_out,
        saved[0, 0, 0],
        w_gate[0, 0],
        w_up[0, 0],
        w_down[0, 0],
        probe[0, 0],
    )
    return found[None, None]


def solution(mesh):
    return jax.shard_map(
        per_device,
        mesh=mesh,
        in_specs=(
            P(("expert", "dp"), None),
            P("pipe", ("expert", "dp"), None),
            P("pipe", ("expert", "dp"), None),
            P("pipe", "expert", "dp", None, None, None, None),
            P("pipe", "expert", None, None),
            P("pipe", "expert", None, None),
            P("pipe", "expert", None, None),
            P("pipe", "expert", None, None),
        ),
        out_specs=P("pipe", "expert", "dp", None),
        check_vma=False,
    )
```

time: 1190 us -> 367 us (0.31)
  waiting for transfers between devices: 522 us -> 0 us
  Pallas kernels: 0 us -> 360 us
  starting transfers between devices: 319 us -> 0 us
  matrix products: 175 us -> 0 us
  local copies, waits for them, and re-layouts: 102 us -> 5.08 us
  other arithmetic: 45.2 us -> 1.6 us
  between operations: 13.4 us -> 0.04 us
    all_to_all x60 -> x0, waiting for transfers between devices: 371 us -> none  [the longest x15 117 us: advance(): lax.all_to_all(send_adjoint, 'expert', split_axis=0, concat_axis=0, tiled...]
    pallas_call x0 -> x1, Pallas kernels: none -> 360 us  [per_device(): pl.pallas_call(functools.partial(relay_kernel, (stages, experts, replicas...]
    all_to_all x60 -> x0, starting transfers between devices: 280 us -> none  [the longest x15 83.3 us: advance(): lax.all_to_all(send_tangent, 'expert', split_axis=0, concat_axis=0, tiled...]
    dot_general x167 -> x0, matrix products: 175 us -> none  [the longest x90 120 us: contract_last(): lax.dot_general(left, right, (((1,), (1,)), ((), ())), preferred_element_...]
    ppermute x30 -> x0, waiting for transfers between devices: 101 us -> none  [passed_along(): lax.ppermute(value, axis, [(source, source + steps) for source in range(f...]
    reshape x120 -> x1, local copies, waits for them, and re-layouts: 51.3 us -> 0.68 us  [pick_tables(): weight = jnp.broadcast_to(probs.reshape(M, T_MB, TOP).transpose(0, 2, 1)[...]
    reduce_scatter x1 -> x0, waiting for transfers between devices: 50.5 us -> none  [per_device(): lax.psum_scatter((contract_first(adjoint_rows, hidden_dot_rows) + contrac...]
    ppermute x30 -> x0, starting transfers between devices: 38.7 us -> none  [passed_along(): lax.ppermute(value, axis, [(source, source + steps) for source in range(f...]
  transfers between devices with their start and end apart: 91 -> 0, of which waited for: 87 -> 0; matrix products, arithmetic and copies ran while one was open for 14% -> 0% of each run, Pallas kernels for 0% -> 0%
where the time goes in v1:
time: 367 us
  Pallas kernels  360 us (98%)
  local copies, waits for them, and re-layouts  5.08 us (1%)
    pallas_call x1, Pallas kernels, per_device(): pl.pallas_call(functools.partial(relay_kernel, (stages, experts, replicas...  360 us

profile of v1, /device:TPU:1, one launch (start us, length us, event | category | flops | bytes accessed | tf_op | source)
XLA Modules:
  0.0 366.5 jit_solution(9250114076567981835)
XLA Ops:
  0.0 0.7 broadcast_multiply_fusion
  0.7 0.1 add.27
  0.8 0.1 add.28
  0.8 0.1 mul.19
  0.9 0.8 reshape_squeeze.4
  1.7 0.7 reshape.31.weight_ref
  2.4 0.8 copy.20
  3.2 0.1 eq.15
  3.3 0.3 convert_reduce_fusion
  3.6 0.1 copy.21
  3.6 0.1 copy.22
  3.8 0.1 add.26
  3.8 0.6 broadcast_add_fusion.target_ref
  4.5 359.8 %relay.1 = f32[512,512]{1,0:T(8,128)} custom-call(s32[8,2,128]{2,1,0:T(2,128)} %broadcast_add_fusion.target_ref, f32[8,2,128]{2,1,0:T(2,128)} %reshape.31.weight_ref, bf16[384,384]{1,0:T(8,128)(2,1)} %constant.8.clone.order_ref.unorder_ref, bf16[384,384]{1,0:T(8,128)(2,1)} %constant.8.clone.order_ref.unorder_ref, bf16[128,2048]{1,0:T(8,128)(2,1)} %adjoint_ref.1, ...), custom_call_target="tpu_custom_call" | custom-call | tf_op jit(solution)/shard_map/relay/pallas_call | solution.py:427
  364.3 2.3 copy.26
  (7 shorter events, 0.0 us)

commit v2 on v1

v2 whole, which is shorter than its diff:
```python
import functools

import jax
import jax.numpy as jnp
import numpy as np
from jax import lax
from jax.experimental import pallas as pl
from jax.experimental.pallas import tpu as pltpu
from jax.sharding import PartitionSpec as P

M = 8
T_MB = 16
TOP = 2
KINDS = 2
CHUNKS = 2
PARTS = 4
MESH = pl.DeviceIdType.MESH
F32 = jnp.float32
BF16 = jnp.bfloat16


def dot(left, right, dims):
    return lax.dot_general(left, right, (dims, ((), ())), preferred_element_type=F32)


def wait_bytes(view, sem):
    pltpu.make_async_copy(view, view, sem).wait()


def relay_kernel(
    sizes,
    target_ref,
    weight_ref,
    order_ref,
    unorder_ref,
    adjoint_ref,
    saved_ref,
    gate_ref,
    up_ref,
    down_ref,
    probe_ref,
    out_ref,
    target_own,
    weight_own,
    target_above,
    token_in,
    token_now,
    pick_send,
    pick_recv,
    back_send,
    back_recv,
    pick_rows,
    block_rows,
    hidden_rows,
    factors,
    grads,
    total,
    down_turned,
    inner_turned,
    placing_ref,
    merging_ref,
    scale_ref,
    table_send_sem,
    table_recv_sem,
    token_send_sem,
    token_recv_sem,
    pick_send_sem,
    pick_recv_sem,
    back_send_sem,
    back_recv_sem,
    block_send_sem,
    block_recv_sem,
    hidden_send_sem,
    hidden_recv_sem,
):
    stages, experts, replicas, capacity = sizes
    stage = lax.axis_index("pipe")
    expert = lax.axis_index("expert")
    replica = lax.axis_index("dp")
    below = lax.rem(stage + stages - 1, stages)
    above = lax.rem(stage + 1, stages)
    is_top = stage == stages - 1
    is_bottom = stage == 0
    adds_own = stage == stages // 2
    gets_sums = stage == stages // 2 - 1
    back_stage = jnp.where(adds_own, stage, below)
    is_lower = stage < stages // 2
    mirror = experts - 1 - expert
    source = jnp.where(is_lower, mirror, expert)
    expert_below = jnp.where(adds_own, mirror, expert)
    slots = experts * capacity
    wire = PARTS * capacity
    lanes = pick_send.shape[-1]
    span = PARTS * lanes
    width = gate_ref.shape[1]
    block_parts = CHUNKS * PARTS // replicas
    block = block_parts * slots

    expert_peers = [lax.rem(expert + step, experts) for step in range(experts)]
    replica_peers = [lax.rem(replica + step, replicas) for step in range(replicas)]

    barrier = pltpu.get_barrier_semaphore()

    def greet(peer, carry):
        for other in (below, above):
            pl.semaphore_signal(
                barrier, inc=1, device_id={"pipe": other, "expert": peer}, device_id_type=MESH
            )
        return carry

    lax.fori_loop(0, experts, greet, 0)
    for step in range(1, experts):
        pl.semaphore_signal(
            barrier,
            inc=1,
            device_id={"expert": expert_peers[step]},
            device_id_type=MESH,
        )
    for step in range(1, replicas):
        pl.semaphore_signal(
            barrier,
            inc=1,
            device_id={"dp": replica_peers[step]},
            device_id_type=MESH,
        )
    pl.semaphore_wait(barrier, 2 * experts + experts - 1 + replicas - 1)

    def table_copy(source_ref, landing_ref, index, device):
        return pltpu.make_async_remote_copy(
            src_ref=source_ref,
            dst_ref=landing_ref,
            send_sem=table_send_sem.at[index],
            recv_sem=table_recv_sem.at[index],
            device_id=device,
            device_id_type=MESH,
        )

    below_copy = table_copy(
        target_ref,
        target_above,
        0,
        {"pipe": below, "expert": jnp.where(stage <= stages // 2, mirror, expert)},
    )
    mirror_copies = [
        table_copy(target_ref, target_own, 1, {"expert": mirror}),
        table_copy(weight_ref, weight_own, 2, {"expert": mirror}),
    ]

    @pl.when(jnp.logical_not(is_bottom))
    def _():
        below_copy.start()

    @pl.when(is_lower)
    def _():
        for copy in mirror_copies:
            copy.start()
        for copy in mirror_copies:
            copy.wait_recv()

    @pl.when(jnp.logical_not(is_lower))
    def _():
        target_own[...] = target_ref[...]
        weight_own[...] = weight_ref[...]

    @pl.when(jnp.logical_not(is_top))
    def _():
        below_copy.wait_recv()

    rows = lax.broadcasted_iota(jnp.int32, (experts * wire, PARTS * T_MB), 0)

    def matches(table, micro):
        pair_rows = table[micro]
        return rows == pair_rows[0:1, :], rows == pair_rows[1:2, :]

    def onehot(first, second):
        return jnp.where(first | second, 1.0, 0.0).astype(BF16)

    def curvature(micro, kind):
        if kind == 0:
            wait_bytes(hidden_rows.at[micro, :, pl.ds(0, replicas - 1)], hidden_recv_sem.at[micro])
        wait_bytes(block_rows.at[micro, kind], block_recv_sem.at[micro, kind])
        right = hidden_rows[micro, kind].reshape(replicas * slots, width)
        for part in range(block_parts):
            left = block_rows[micro, kind, :, part * slots : (part + 1) * slots, :]
            found = dot(left.reshape(replicas * slots, lanes), right, ((0,), (0,)))
            here = slice(part * lanes, (part + 1) * lanes)
            total[here, :] = total[here, :] + found

    def merge(merging, base, micro, kind, chunk):
        wait_bytes(back_recv.at[micro, kind, chunk], back_recv_sem.at[micro, kind, chunk])
        returned = back_recv[micro, kind, chunk].reshape(experts * wire, lanes)
        token_now[micro, kind, chunk] = (
            base.astype(F32) + dot(merging, returned, ((0,), (0,)))
        ).astype(BF16)

    def forward(micro, kind, chunk):
        pltpu.make_async_remote_copy(
            src_ref=token_now.at[micro, kind, chunk],
            dst_ref=token_in.at[micro, kind, chunk],
            send_sem=token_send_sem.at[micro],
            recv_sem=token_recv_sem.at[micro, kind, chunk],
            device_id={"pipe": below, "expert": expert_below},
            device_id_type=MESH,
        ).start()

    def add_own(micro, kind):
        merging = onehot(*matches(target_own, micro))
        for chunk in range(CHUNKS):
            merge(merging, token_now[micro, kind, chunk], micro, kind, chunk)
            forward(micro, kind, chunk)

    def tables(micro):
        first, second = matches(target_own, micro)
        weights = weight_own[micro]
        placing_ref[...] = onehot(first, second)
        scale_ref[...] = jnp.broadcast_to(
            jnp.sum(
                jnp.where(first, weights[0:1, :], 0.0) + jnp.where(second, weights[1:2, :], 0.0),
                axis=1,
                keepdims=True,
            ),
            scale_ref.shape,
        )
        merging_ref[...] = onehot(*matches(target_above, micro))

    def hand_out(micro, kind):
        for chunk in range(CHUNKS):

            @pl.when(is_top)
            def _():
                row_start = pl.multiple_of(micro * T_MB, T_MB)
                for part in range(PARTS):
                    start = chunk * span + part * lanes
                    base = part * T_MB
                    if kind == 0:
                        piece = adjoint_ref[pl.ds(row_start, T_MB), start : start + lanes]
                    else:
                        piece = jnp.zeros((T_MB, lanes), BF16)
                    token_now[micro, kind, chunk, base : base + T_MB, :] = piece

            @pl.when(jnp.logical_not(is_top))
            def _():
                wait_bytes(token_in.at[micro, kind, chunk], token_recv_sem.at[micro, kind, chunk])

            @pl.when(gets_sums)
            def _():
                token_now[micro, kind, chunk] = token_in[micro, kind, chunk]

            @pl.when(jnp.logical_not(is_top | gets_sums))
            def _():
                merge(merging_ref[...], token_in[micro, kind, chunk], micro, kind, chunk)

            picked = dot(placing_ref[...], token_now[micro, kind, chunk], ((1,), (0,)))
            picked = picked * scale_ref[...]
            pick_send[micro, kind, chunk] = picked.astype(BF16).reshape(experts, wire, lanes)
            for step in range(1, experts):
                peer = expert_peers[step]
                pltpu.make_async_remote_copy(
                    src_ref=pick_send.at[micro, kind, chunk, peer],
                    dst_ref=pick_recv.at[micro, kind, chunk, source],
                    send_sem=pick_send_sem.at[micro],
                    recv_sem=pick_recv_sem.at[micro, kind, chunk],
                    device_id={"expert": peer},
                    device_id_type=MESH,
                ).start()
            pltpu.make_async_copy(
                pick_send.at[micro, kind, chunk, expert],
                pick_recv.at[micro, kind, chunk, source],
                pick_recv_sem.at[micro, kind, chunk],
            ).start()

            @pl.when(jnp.logical_not(is_bottom | adds_own))
            def _():
                forward(micro, kind, chunk)

    def activations(micro):
        pre_gate = saved_ref[micro, 0].astype(F32)
        pre_up = saved_ref[micro, 1].astype(F32)
        tangent_gate = saved_ref[micro, 2].astype(F32)
        tangent_up = saved_ref[micro, 3].astype(F32)
        sigmoid = jax.nn.sigmoid(pre_gate)
        silu = pre_gate * sigmoid
        slope = sigmoid * (1.0 + pre_gate * (1.0 - sigmoid))
        bend = sigmoid * (1.0 - sigmoid) * (2.0 + pre_gate * (1.0 - 2.0 * sigmoid))
        hidden_rows[micro, 0, replica] = (
            slope * tangent_gate * pre_up + silu * tangent_up
        ).astype(BF16)
        hidden_rows[micro, 1, replica] = (silu * pre_up).astype(BF16)
        for step in range(1, replicas):
            pltpu.make_async_remote_copy(
                src_ref=hidden_rows.at[micro, :, replica],
                dst_ref=hidden_rows.at[micro, :, replica],
                send_sem=hidden_send_sem.at[micro],
                recv_sem=hidden_recv_sem.at[micro],
                device_id={"dp": replica_peers[step]},
                device_id_type=MESH,
            ).start()
        factors[0] = pre_up * slope
        factors[1] = silu
        factors[2] = tangent_up * slope + pre_up * bend * tangent_gate
        factors[3] = slope * tangent_gate

    def side_by_side(ordered):
        return jnp.concatenate(
            [ordered[part * slots : (part + 1) * slots, :] for part in range(PARTS)], axis=1
        )

    def take_in(micro, kind):
        for chunk in range(CHUNKS):
            columns = slice(chunk * span, (chunk + 1) * span)
            wait_bytes(pick_recv.at[micro, kind, chunk], pick_recv_sem.at[micro, kind, chunk])
            received = pick_recv[micro, kind, chunk].reshape(experts * wire, lanes)
            ordered = dot(order_ref[...], received, ((1,), (0,))).astype(BF16)
            pick_rows[micro, kind, chunk] = ordered

            @pl.when(jnp.logical_not(is_bottom))
            def _():
                main = dot(side_by_side(ordered), down_turned[columns, :], ((1,), (0,)))
                if chunk == 0:
                    grads[kind] = main + grads[1] if kind == 1 else main
                else:
                    grads[kind] = grads[kind] + main

            for step in range(replicas):
                peer = replica_peers[step]
                first_part = peer * block_parts
                rows_out = pick_rows.at[
                    micro, kind, chunk, pl.ds(lax.rem(first_part, PARTS) * slots, block)
                ]
                landing = block_rows.at[micro, kind, replica]

                @pl.when(lax.div(first_part, PARTS) == chunk)
                def _():
                    if step == 0:
                        pltpu.make_async_copy(
                            rows_out, landing, block_recv_sem.at[micro, kind]
                        ).start()
                    else:
                        pltpu.make_async_remote_copy(
                            src_ref=rows_out,
                            dst_ref=landing,
                            send_sem=block_send_sem.at[micro],
                            recv_sem=block_recv_sem.at[micro, kind],
                            device_id={"dp": peer},
                            device_id_type=MESH,
                        ).start()

    def hand_back(micro, kind):
        grad = grads[0]
        if kind == 0:
            left = [grad * factors[0], grad * factors[1]]
        else:
            grad_dot = grads[1]
            left = [
                grad_dot * factors[0] + grad * factors[2],
                grad_dot * factors[1] + grad * factors[3],
            ]
        left = jnp.concatenate([piece.astype(BF16) for piece in left], axis=1)
        for chunk in range(CHUNKS):
            columns = slice(chunk * span, (chunk + 1) * span)
            back = dot(left, inner_turned[:, columns], ((1,), (0,))).astype(BF16)
            stacked = jnp.concatenate(
                [back[:, part * lanes : (part + 1) * lanes] for part in range(PARTS)], axis=0
            )
            back_send[micro, kind, chunk] = (
                dot(unorder_ref[...], stacked, ((1,), (0,)))
                .astype(BF16)
                .reshape(experts, wire, lanes)
            )
            for step in range(1, experts + 1):
                peer = expert_peers[step % experts]
                copy = pltpu.make_async_remote_copy(
                    src_ref=back_send.at[
                        micro, kind, chunk, jnp.where(is_lower, experts - 1 - peer, peer)
                    ],
                    dst_ref=back_recv.at[micro, kind, chunk, expert],
                    send_sem=back_send_sem.at[micro],
                    recv_sem=back_recv_sem.at[micro, kind, chunk],
                    device_id={"pipe": back_stage, "expert": peer},
                    device_id_type=MESH,
                )
                if step < experts:
                    copy.start()
                else:
                    pl.when(jnp.logical_not(adds_own))(copy.start)

                    @pl.when(adds_own)
                    def _():
                        pltpu.make_async_copy(
                            back_send.at[micro, kind, chunk, expert],
                            back_recv.at[micro, kind, chunk, expert],
                            back_recv_sem.at[micro, kind, chunk],
                        ).start()

    total[...] = jnp.zeros_like(total)

    def turn_weights():
        side = min(256, down_ref.shape[1])

        def turn_down(index, carry):
            here = pl.ds(pl.multiple_of(index * side, side), side)
            down_turned[here, :] = down_ref[:, here].T
            inner_turned[0:width, here] = gate_ref[here, :].T
            inner_turned[width : 2 * width, here] = up_ref[here, :].T
            return carry

        lax.fori_loop(0, down_ref.shape[1] // side, turn_down, 0)

    def aside(micro):
        for chunk in range(CHUNKS):
            found = dot(
                side_by_side(pick_rows[micro, 0, chunk]),
                probe_ref[chunk * span : (chunk + 1) * span, :],
                ((1,), (0,)),
            )
            grads[1] = found if chunk == 0 else grads[1] + found

    def advance(micro, carry):
        hand_out(micro, 0)
        hand_out(micro, 1)

        @pl.when(is_top & (micro == 0))
        def _():
            turn_weights()

        activations(micro)

        @pl.when(micro > 0)
        def _():
            curvature(micro - 1, 0)
            curvature(micro - 1, 1)

        @pl.when(micro < M - 1)
        def _():
            tables(micro + 1)

        take_in(micro, 0)

        @pl.when(jnp.logical_not(is_bottom))
        def _():
            hand_back(micro, 0)
            aside(micro)

        @pl.when(micro == M - 1)
        def _():
            curvature(micro, 0)

        take_in(micro, 1)

        @pl.when(jnp.logical_not(is_bottom))
        def _():
            hand_back(micro, 1)

        @pl.when(adds_own)
        def _():
            add_own(micro, 0)
            add_own(micro, 1)

        return carry

    tables(0)

    @pl.when(jnp.logical_not(is_top))
    def _():
        turn_weights()

    lax.fori_loop(0, M, advance, 0)
    curvature(M - 1, 1)
    rows_here = block_parts * lanes
    start = pl.multiple_of(replica * rows_here, rows_here)
    out_ref[...] = probe_ref[pl.ds(start, rows_here), :].astype(F32) * total[...]

    def settle(micro, carry):
        wait_bytes(pick_send.at[micro, :, :, pl.ds(0, experts - 1)], pick_send_sem.at[micro])
        wait_bytes(hidden_rows.at[micro, :, pl.ds(0, replicas - 1)], hidden_send_sem.at[micro])
        wait_bytes(block_rows.at[micro, :, pl.ds(0, replicas - 1)], block_send_sem.at[micro])

        @pl.when(jnp.logical_not(is_bottom))
        def _():
            wait_bytes(token_now.at[micro], token_send_sem.at[micro])

        @pl.when(jnp.logical_not(is_bottom | adds_own))
        def _():
            wait_bytes(back_send.at[micro], back_send_sem.at[micro])

        @pl.when(adds_own)
        def _():
            wait_bytes(back_send.at[micro, :, :, pl.ds(0, experts - 1)], back_send_sem.at[micro])

        return carry

    lax.fori_loop(0, M, settle, 0)

    @pl.when(jnp.logical_not(is_bottom))
    def _():
        below_copy.wait_send()

    @pl.when(is_lower)
    def _():
        for copy in mirror_copies:
            copy.wait_send()


def row_orders(experts, capacity):
    slots = experts * capacity
    order = np.zeros((PARTS * slots, PARTS * slots), np.float32)
    for part in range(PARTS):
        for source in range(experts):
            for slot in range(capacity):
                order[
                    part * slots + source * capacity + slot,
                    (source * PARTS + part) * capacity + slot,
                ] = 1.0
    return order


def pick_tables(routes, probs, capacity):
    picks = T_MB * TOP
    flat = routes.reshape(M, picks)
    index = jnp.arange(picks, dtype=jnp.int32)
    earlier = index[None, :] < index[:, None]
    same = flat[:, :, None] == flat[:, None, :]
    position = jnp.sum((same & earlier[None]).astype(jnp.int32), axis=2)
    base = (flat * (PARTS * capacity) + position).reshape(M, T_MB, TOP).transpose(0, 2, 1)
    offset = jnp.arange(PARTS, dtype=jnp.int32) * capacity
    target = (base[:, :, None, :] + offset[None, None, :, None]).reshape(M, TOP, PARTS * T_MB)
    weight = jnp.broadcast_to(
        probs.reshape(M, T_MB, TOP).transpose(0, 2, 1)[:, :, None, :], (M, TOP, PARTS, T_MB)
    ).reshape(M, TOP, PARTS * T_MB)
    return target, weight


def per_device(adjoint_out, gate_probs, routes, saved, w_gate, w_up, w_down, probe):
    stages = lax.axis_size("pipe")
    experts = lax.axis_size("expert")
    replicas = lax.axis_size("dp")
    slots = saved.shape[5]
    capacity = slots // experts
    model = adjoint_out.shape[1]
    width = w_gate.shape[3]
    lanes = model // PARTS // CHUNKS
    wire = PARTS * capacity
    tokens = PARTS * T_MB
    block = CHUNKS * PARTS // replicas * slots
    target, weight = pick_tables(routes[0], gate_probs[0], capacity)
    order = row_orders(experts, capacity)
    vmem = pl.BlockSpec(memory_space=pltpu.VMEM)
    dma = pltpu.SemaphoreType.DMA
    found = pl.pallas_call(
        functools.partial(relay_kernel, (stages, experts, replicas, capacity)),
        out_shape=jax.ShapeDtypeStruct((model // replicas, width), F32),
        in_specs=[vmem] * 10,
        out_specs=vmem,
        scratch_shapes=[
            pltpu.VMEM((M, TOP, tokens), jnp.int32),
            pltpu.VMEM((M, TOP, tokens), F32),
            pltpu.VMEM((M, TOP, tokens), jnp.int32),
            pltpu.VMEM((M, KINDS, CHUNKS, tokens, lanes), BF16),
            pltpu.VMEM((M, KINDS, CHUNKS, tokens, lanes), BF16),
            pltpu.VMEM((M, KINDS, CHUNKS, experts, wire, lanes), BF16),
            pltpu.VMEM((M, KINDS, CHUNKS, experts, wire, lanes), BF16),
            pltpu.VMEM((M, KINDS, CHUNKS, experts, wire, lanes), BF16),
            pltpu.VMEM((M, KINDS, CHUNKS, experts, wire, lanes), BF16),
            pltpu.VMEM((M, KINDS, CHUNKS, PARTS * slots, lanes), BF16),
            pltpu.VMEM((M, KINDS, replicas, block, lanes), BF16),
            pltpu.VMEM((M, KINDS, replicas, slots, width), BF16),
            pltpu.VMEM((4, slots, width), F32),
            pltpu.VMEM((2, slots, width), F32),
            pltpu.VMEM((model // replicas, width), F32),
            pltpu.VMEM((model, width), BF16),
            pltpu.VMEM((2 * width, model), BF16),
            pltpu.VMEM((experts * wire, tokens), BF16),
            pltpu.VMEM((experts * wire, tokens), BF16),
            pltpu.VMEM((experts * wire, lanes), F32),
            dma((3,)),
            dma((3,)),
            dma((M,)),
            dma((M, KINDS, CHUNKS)),
            dma((M,)),
            dma((M, KINDS, CHUNKS)),
            dma((M,)),
            dma((M, KINDS, CHUNKS)),
            dma((M,)),
            dma((M, KINDS)),
            dma((M,)),
            dma((M,)),
        ],
        compiler_params=pltpu.CompilerParams(
            collective_id=0, has_side_effects=True, vmem_limit_bytes=60 * 1024 * 1024
        ),
        name="relay",
    )(
        target,
        weight,
        jnp.asarray(order, BF16),
        jnp.asarray(order.T, BF16),
        adjoint_out,
        saved[0, 0, 0],
        w_gate[0, 0],
        w_up[0, 0],
        w_down[0, 0],
        probe[0, 0],
    )
    return found[None, None]


def solution(mesh):
    return jax.shard_map(
        per_device,
        mesh=mesh,
        in_specs=(
            P(("expert", "dp"), None),
            P("pipe", ("expert", "dp"), None),
            P("pipe", ("expert", "dp"), None),
            P("pipe", "expert", "dp", None, None, None, None),
            P("pipe", "expert", None, None),
            P("pipe", "expert", None, None),
            P("pipe", "expert", None, None),
            P("pipe", "expert", None, None),
        ),
        out_specs=P("pipe", "expert", "dp", None),
        check_vma=False,
    )
```

time: 367 us -> 298 us (0.81)
  Pallas kernels: 360 us -> 291 us
    pallas_call x1, Pallas kernels: 360 us -> 291 us  [per_device(): pl.pallas_call(functools.partial(relay_kernel, (stages, experts, replicas...]
where the time goes in v2:
time: 298 us
  Pallas kernels  291 us (98%)
  local copies, waits for them, and re-layouts  5.09 us (2%)
    pallas_call x1, Pallas kernels, per_device(): pl.pallas_call(functools.partial(relay_kernel, (stages, experts, replicas...  291 us

profile of v2, /device:TPU:1, one launch (start us, length us, event | category | flops | bytes accessed | tf_op | source)
XLA Modules:
  0.0 297.6 jit_solution(910906606079664373)
XLA Ops:
  0.0 0.7 broadcast_multiply_fusion
  0.7 0.1 add.27
  0.8 0.1 add.28
  0.8 0.1 mul.19
  0.9 0.8 reshape_squeeze.4
  1.7 0.7 reshape.31.weight_ref
  2.4 0.8 copy.20
  3.2 0.1 eq.15
  3.3 0.3 convert_reduce_fusion
  3.6 0.1 copy.21
  3.6 0.1 copy.22
  3.8 0.1 add.26
  3.9 0.6 broadcast_add_fusion.target_ref
  4.5 290.9 %relay.1 = f32[512,512]{1,0:T(8,128)} custom-call(s32[8,2,64]{2,1,0:T(2,128)} %broadcast_add_fusion.target_ref, f32[8,2,64]{2,1,0:T(2,128)} %reshape.31.weight_ref, bf16[192,192]{1,0:T(8,128)(2,1)} %constant.10.clone.order_ref, bf16[192,192]{1,0:T(8,128)(2,1)} %constant.11.clone.unorder_ref, bf16[128,2048]{1,0:T(8,128)(2,1)} %adjoint_ref.1, ...), custom_call_target="tpu_custom_call" | custom-call | tf_op jit(solution)/shard_map/relay/pallas_call | solution.py:549
  295.4 2.3 copy.26
  (7 shorter events, 0.0 us)

commit v3 on v2

--- a/solution.py
+++ b/solution.py
@@ -23,23 +23,40 @@
     return lax.dot_general(left, right, (dims, ((), ())), preferred_element_type=F32)
 
 
+def partner_order(experts):
+    half, quarter = experts // 2, experts // 4
+    if quarter == 0:
+        return list(range(experts - 1, -1, -1))
+    far = list(range(experts - 1, half - 1, -1))
+    near = list(range(half - 1, -1, -1))
+    return far[:quarter] + near[:quarter] + far[quarter:] + near[quarter:]
+
+
 def wait_bytes(view, sem):
     pltpu.make_async_copy(view, view, sem).wait()
 
 
 def relay_kernel(
     sizes,
-    target_ref,
-    weight_ref,
+    routes_ref,
+    probs_ref,
     order_ref,
     unorder_ref,
+    adjoint_far,
+    saved_far,
+    gate_far,
+    up_far,
+    down_far,
+    probe_far,
+    out_ref,
     adjoint_ref,
     saved_ref,
     gate_ref,
     up_ref,
     down_ref,
     probe_ref,
-    out_ref,
+    target_ref,
+    weight_ref,
     target_own,
     weight_own,
     target_above,
@@ -60,6 +77,7 @@
     placing_ref,
     merging_ref,
     scale_ref,
+    load_sem,
     table_send_sem,
     table_recv_sem,
     token_send_sem,
@@ -83,6 +101,8 @@
     is_bottom = stage == 0
     adds_own = stage == stages // 2
     gets_sums = stage == stages // 2 - 1
+    is_late = stage > stages // 2
+    ends_apart = stage >= stages // 2 - 1
     back_stage = jnp.where(adds_own, stage, below)
     is_lower = stage < stages // 2
     mirror = experts - 1 - expert
@@ -96,7 +116,23 @@
     block_parts = CHUNKS * PARTS // replicas
     block = block_parts * slots
 
-    expert_peers = [lax.rem(expert + step, experts) for step in range(experts)]
+    loads = [
+        pltpu.make_async_copy(far, near, load_sem.at[index])
+        for index, (far, near) in enumerate(
+            [
+                (adjoint_far, adjoint_ref),
+                (down_far, down_ref),
+                (gate_far, gate_ref),
+                (up_far, up_ref),
+                (saved_far, saved_ref),
+                (probe_far, probe_ref),
+            ]
+        )
+    ]
+    for load in loads:
+        load.start()
+
+    expert_peers = [expert ^ k for k in partner_order(experts)]
     replica_peers = [lax.rem(replica + step, replicas) for step in range(replicas)]
 
     barrier = pltpu.get_barrier_semaphore()
@@ -109,7 +145,7 @@
         return carry
 
     lax.fori_loop(0, experts, greet, 0)
-    for step in range(1, experts):
+    for step in range(experts - 1):
         pl.semaphore_signal(
             barrier,
             inc=1,
@@ -123,6 +159,7 @@
             device_id={"dp": replica_peers[step]},
             device_id_type=MESH,
         )
+    set_tables(routes_ref, probs_ref, target_ref, weight_ref, capacity)
     pl.semaphore_wait(barrier, 2 * experts + experts - 1 + replicas - 1)
 
     def table_copy(source_ref, landing_ref, index, device):
@@ -169,8 +206,8 @@
     rows = lax.broadcasted_iota(jnp.int32, (experts * wire, PARTS * T_MB), 0)
 
     def matches(table, micro):
-        pair_rows = table[micro]
-        return rows == pair_rows[0:1, :], rows == pair_rows[1:2, :]
+        here = pl.ds(micro, 1)
+        return rows == table[0, here, :], rows == table[1, here, :]
 
     def onehot(first, second):
         return jnp.where(first | second, 1.0, 0.0).astype(BF16)
@@ -211,17 +248,38 @@
 
     def tables(micro):
         first, second = matches(target_own, micro)
-        weights = weight_own[micro]
+        here = pl.ds(micro, 1)
         placing_ref[...] = onehot(first, second)
         scale_ref[...] = jnp.broadcast_to(
             jnp.sum(
-                jnp.where(first, weights[0:1, :], 0.0) + jnp.where(second, weights[1:2, :], 0.0),
+                jnp.where(first, weight_own[0, here, :], 0.0)
+                + jnp.where(second, weight_own[1, here, :], 0.0),
                 axis=1,
                 keepdims=True,
             ),
             scale_ref.shape,
         )
         merging_ref[...] = onehot(*matches(target_above, micro))
+
+    def send_picks(micro, kind, chunk):
+        picked = dot(placing_ref[...], token_now[micro, kind, chunk], ((1,), (0,)))
+        picked = picked * scale_ref[...]
+        pick_send[micro, kind, chunk] = picked.astype(BF16).reshape(experts, wire, lanes)
+        for step in range(experts - 1):
+            peer = expert_peers[step]
+            pltpu.make_async_remote_copy(
+                src_ref=pick_send.at[micro, kind, chunk, peer],
+                dst_ref=pick_recv.at[micro, kind, chunk, source],
+                send_sem=pick_send_sem.at[micro],
+                recv_sem=pick_recv_sem.at[micro, kind, chunk],
+                device_id={"expert": peer},
+                device_id_type=MESH,
+            ).start()
+        pltpu.make_async_copy(
+            pick_send.at[micro, kind, chunk, expert],
+            pick_recv.at[micro, kind, chunk, source],
+            pick_recv_sem.at[micro, kind, chunk],
+        ).start()
 
     def hand_out(micro, kind):
         for chunk in range(CHUNKS):
@@ -250,24 +308,12 @@
             def _():
                 merge(merging_ref[...], token_in[micro, kind, chunk], micro, kind, chunk)
 
-            picked = dot(placing_ref[...], token_now[micro, kind, chunk], ((1,), (0,)))
-            picked = picked * scale_ref[...]
-            pick_send[micro, kind, chunk] = picked.astype(BF16).reshape(experts, wire, lanes)
-            for step in range(1, experts):
-                peer = expert_peers[step]
-                pltpu.make_async_remote_copy(
-                    src_ref=pick_send.at[micro, kind, chunk, peer],
-                    dst_ref=pick_recv.at[micro, kind, chunk, source],
-                    send_sem=pick_send_sem.at[micro],
-                    recv_sem=pick_recv_sem.at[micro, kind, chunk],
-                    device_id={"expert": peer},
-                    device_id_type=MESH,
-                ).start()
-            pltpu.make_async_copy(
-                pick_send.at[micro, kind, chunk, expert],
-                pick_recv.at[micro, kind, chunk, source],
-                pick_recv_sem.at[micro, kind, chunk],
-            ).start()
+            if kind == 0:
+                send_picks(micro, kind, chunk)
+            else:
+                pl.when(jnp.logical_not(is_top))(
+                    functools.partial(send_picks, micro, kind, chunk)
+                )
 
             @pl.when(jnp.logical_not(is_bottom | adds_own))
             def _():
@@ -281,7 +327,10 @@
         sigmoid = jax.nn.sigmoid(pre_gate)
         silu = pre_gate * sigmoid
         slope = sigmoid * (1.0 + pre_gate * (1.0 - sigmoid))
-        bend = sigmoid * (1.0 - sigmoid) * (2.0 + pre_gate * (1.0 - 2.0 * sigmoid))
+        return pre_gate, pre_up, tangent_gate, tangent_up, sigmoid, silu, slope
+
+    def share_hidden(micro, carry):
+        _, pre_up, tangent_gate, tangent_up, _, silu, slope = activations(micro)
         hidden_rows[micro, 0, replica] = (
             slope * tangent_gate * pre_up + silu * tangent_up
         ).astype(BF16)
@@ -295,6 +344,11 @@
                 device_id={"dp": replica_peers[step]},
                 device_id_type=MESH,
             ).start()
+        return carry
+
+    def set_factors(micro):
+        pre_gate, pre_up, tangent_gate, tangent_up, sigmoid, silu, slope = activations(micro)
+        bend = sigmoid * (1.0 - sigmoid) * (2.0 + pre_gate * (1.0 - 2.0 * sigmoid))
         factors[0] = pre_up * slope
         factors[1] = silu
         factors[2] = tangent_up * slope + pre_up * bend * tangent_gate
@@ -307,43 +361,65 @@
 
     def take_in(micro, kind):
         for chunk in range(CHUNKS):
-            columns = slice(chunk * span, (chunk + 1) * span)
-            wait_bytes(pick_recv.at[micro, kind, chunk], pick_recv_sem.at[micro, kind, chunk])
-            received = pick_recv[micro, kind, chunk].reshape(experts * wire, lanes)
-            ordered = dot(order_ref[...], received, ((1,), (0,))).astype(BF16)
-            pick_rows[micro, kind, chunk] = ordered
-
-            @pl.when(jnp.logical_not(is_bottom))
+            if kind == 0:
+                take_chunk(micro, kind, chunk)
+            else:
+                pl.when(jnp.logical_not(is_top))(
+                    functools.partial(take_chunk, micro, kind, chunk)
+                )
+
+                @pl.when(is_top)
+                def _():
+                    pick_rows[micro, kind, chunk] = jnp.zeros((PARTS * slots, lanes), BF16)
+
+    def take_chunk(micro, kind, chunk):
+        columns = slice(chunk * span, (chunk + 1) * span)
+        wait_bytes(pick_recv.at[micro, kind, chunk], pick_recv_sem.at[micro, kind, chunk])
+        received = pick_recv[micro, kind, chunk].reshape(experts * wire, lanes)
+        ordered = dot(order_ref[...], received, ((1,), (0,))).astype(BF16)
+        pick_rows[micro, kind, chunk] = ordered
+
+        @pl.when(is_bottom)
+        def _():
+            share_rows(micro, kind, chunk)
+
+        @pl.when(jnp.logical_not(is_bottom))
+        def _():
+            main = dot(side_by_side(ordered), down_turned[columns, :], ((1,), (0,)))
+            if chunk == 0:
+                grads[kind] = main + grads[1] if kind == 1 else main
+            else:
+                grads[kind] = grads[kind] + main
+
+    def share_rows(micro, kind, chunk):
+        for step in range(replicas):
+            peer = replica_peers[step]
+            first_part = peer * block_parts
+            rows_out = pick_rows.at[
+                micro, kind, chunk, pl.ds(lax.rem(first_part, PARTS) * slots, block)
+            ]
+            landing = block_rows.at[micro, kind, replica]
+
+            @pl.when(lax.div(first_part, PARTS) == chunk)
             def _():
-                main = dot(side_by_side(ordered), down_turned[columns, :], ((1,), (0,)))
-                if chunk == 0:
-                    grads[kind] = main + grads[1] if kind == 1 else main
+                if step == 0:
+                    pltpu.make_async_copy(
+                        rows_out, landing, block_recv_sem.at[micro, kind]
+                    ).start()
                 else:
-                    grads[kind] = grads[kind] + main
-
-            for step in range(replicas):
-                peer = replica_peers[step]
-                first_part = peer * block_parts
-                rows_out = pick_rows.at[
-                    micro, kind, chunk, pl.ds(lax.rem(first_part, PARTS) * slots, block)
-                ]
-                landing = block_rows.at[micro, kind, replica]
-
-                @pl.when(lax.div(first_part, PARTS) == chunk)
-                def _():
-                    if step == 0:
-                        pltpu.make_async_copy(
-                            rows_out, landing, block_recv_sem.at[micro, kind]
-                        ).start()
-                    else:
-                        pltpu.make_async_remote_copy(
-                            src_ref=rows_out,
-                            dst_ref=landing,
-                            send_sem=block_send_sem.at[micro],
-                            recv_sem=block_recv_sem.at[micro, kind],
-                            device_id={"dp": peer},
-                            device_id_type=MESH,
-                        ).start()
+                    pltpu.make_async_remote_copy(
+                        src_ref=rows_out,
+                        dst_ref=landing,
+                        send_sem=block_send_sem.at[micro],
+                        recv_sem=block_recv_sem.at[micro, kind],
+                        device_id={"dp": peer},
+                        device_id_type=MESH,
+                    ).start()
+
+    def share_all_rows(micro):
+        for kind in range(KINDS):
+            for chunk in range(CHUNKS):
+                share_rows(micro, kind, chunk)
 
     def hand_back(micro, kind):
         grad = grads[0]
@@ -367,8 +443,8 @@
                 .astype(BF16)
                 .reshape(experts, wire, lanes)
             )
-            for step in range(1, experts + 1):
-                peer = expert_peers[step % experts]
+            for step in range(experts):
+                peer = expert_peers[step]
                 copy = pltpu.make_async_remote_copy(
                     src_ref=back_send.at[
                         micro, kind, chunk, jnp.where(is_lower, experts - 1 - peer, peer)
@@ -379,7 +455,7 @@
                     device_id={"pipe": back_stage, "expert": peer},
                     device_id_type=MESH,
                 )
-                if step < experts:
+                if step < experts - 1:
                     copy.start()
                 else:
                     pl.when(jnp.logical_not(adds_own))(copy.start)
@@ -395,6 +471,8 @@
     total[...] = jnp.zeros_like(total)
 
     def turn_weights():
+        for load in loads[1:]:
+            load.wait()
         side = min(256, down_ref.shape[1])
 
         def turn_down(index, carry):
@@ -423,9 +501,9 @@
         def _():
             turn_weights()
 
-        activations(micro)
-
-        @pl.when(micro > 0)
+        set_factors(micro)
+
+        @pl.when((micro > 0) & jnp.logical_not(ends_apart))
         def _():
             curvature(micro - 1, 0)
             curvature(micro - 1, 1)
@@ -441,7 +519,7 @@
             hand_back(micro, 0)
             aside(micro)
 
-        @pl.when(micro == M - 1)
+        @pl.when(is_bottom & (micro == M - 1))
         def _():
             curvature(micro, 0)
 
@@ -450,6 +528,10 @@
         @pl.when(jnp.logical_not(is_bottom))
         def _():
             hand_back(micro, 1)
+
+        @pl.when(jnp.logical_not(is_bottom | ends_apart))
+        def _():
+            share_all_rows(micro)
 
         @pl.when(adds_own)
         def _():
@@ -459,19 +541,57 @@
         return carry
 
     tables(0)
+    loads[0].wait()
 
     @pl.when(jnp.logical_not(is_top))
     def _():
         turn_weights()
 
+    @pl.when(jnp.logical_not(is_late))
+    def _():
+        lax.fori_loop(0, M, share_hidden, 0)
+
     lax.fori_loop(0, M, advance, 0)
-    curvature(M - 1, 1)
+
+    @pl.when(is_late)
+    def _():
+        lax.fori_loop(0, M, share_hidden, 0)
+
+    @pl.when(ends_apart)
+    def _():
+        def share_late(micro, carry):
+            share_all_rows(micro)
+            return carry
+
+        def add_late(micro, carry):
+            curvature(micro, 0)
+            curvature(micro, 1)
+            return carry
+
+        lax.fori_loop(0, M, share_late, 0)
+        lax.fori_loop(0, M, add_late, 0)
+
+    @pl.when(jnp.logical_not(is_bottom | ends_apart))
+    def _():
+        curvature(M - 1, 0)
+
+    @pl.when(jnp.logical_not(ends_apart))
+    def _():
+        curvature(M - 1, 1)
+
     rows_here = block_parts * lanes
     start = pl.multiple_of(replica * rows_here, rows_here)
     out_ref[...] = probe_ref[pl.ds(start, rows_here), :].astype(F32) * total[...]
 
     def settle(micro, carry):
-        wait_bytes(pick_send.at[micro, :, :, pl.ds(0, experts - 1)], pick_send_sem.at[micro])
+        @pl.when(is_top)
+        def _():
+            wait_bytes(pick_send.at[micro, 0, :, pl.ds(0, experts - 1)], pick_send_sem.at[micro])
+
+        @pl.when(jnp.logical_not(is_top))
+        def _():
+            wait_bytes(pick_send.at[micro, :, :, pl.ds(0, experts - 1)], pick_send_sem.at[micro])
+
         wait_bytes(hidden_rows.at[micro, :, pl.ds(0, replicas - 1)], hidden_send_sem.at[micro])
         wait_bytes(block_rows.at[micro, :, pl.ds(0, replicas - 1)], block_send_sem.at[micro])
 
@@ -514,20 +634,49 @@
     return order
 
 
-def pick_tables(routes, probs, capacity):
-    picks = T_MB * TOP
-    flat = routes.reshape(M, picks)
-    index = jnp.arange(picks, dtype=jnp.int32)
-    earlier = index[None, :] < index[:, None]
-    same = flat[:, :, None] == flat[:, None, :]
-    position = jnp.sum((same & earlier[None]).astype(jnp.int32), axis=2)
-    base = (flat * (PARTS * capacity) + position).reshape(M, T_MB, TOP).transpose(0, 2, 1)
-    offset = jnp.arange(PARTS, dtype=jnp.int32) * capacity
-    target = (base[:, :, None, :] + offset[None, None, :, None]).reshape(M, TOP, PARTS * T_MB)
-    weight = jnp.broadcast_to(
-        probs.reshape(M, T_MB, TOP).transpose(0, 2, 1)[:, :, None, :], (M, TOP, PARTS, T_MB)
-    ).reshape(M, TOP, PARTS * T_MB)
-    return target, weight
+def set_tables(routes_ref, probs_ref, target_ref, weight_ref, capacity):
+    count = M * T_MB
+    across = lax.broadcasted_iota(jnp.int32, (count, count), 1)
+    down = lax.broadcasted_iota(jnp.int32, (count, count), 0)
+    same = across == down
+    shift = T_MB.bit_length() - 1
+    earlier = (down < across) & ((down >> shift) == (across >> shift))
+
+    def row_of(column):
+        return jnp.sum(jnp.where(same, column, 0.0), axis=0, keepdims=True)
+
+    columns = [routes_ref[:, k : k + 1].astype(F32) for k in range(TOP)]
+    rows = [row_of(column) for column in columns]
+    wide = (M, count)
+    own = (lax.broadcasted_iota(jnp.int32, wide, 1) >> shift) == lax.broadcasted_iota(
+        jnp.int32, wide, 0
+    )
+    tall = (count, PARTS * T_MB)
+    spread = jnp.where(
+        (lax.broadcasted_iota(jnp.int32, tall, 0) & (T_MB - 1))
+        == (lax.broadcasted_iota(jnp.int32, tall, 1) & (T_MB - 1)),
+        1.0,
+        0.0,
+    ).astype(BF16)
+    part = lax.broadcasted_iota(jnp.int32, (M, PARTS * T_MB), 1) >> shift
+
+    def per_micro(row):
+        return dot(jnp.where(own, row, 0.0).astype(BF16), spread, ((1,), (0,)))
+
+    for k in range(TOP):
+        before = sum(
+            jnp.where(earlier & (column == rows[k]), 1.0, 0.0) for column in columns
+        )
+        position = jnp.sum(before, axis=0, keepdims=True)
+        for other in range(k):
+            position = position + jnp.where(rows[other] == rows[k], 1.0, 0.0)
+        base = per_micro(rows[k] * (PARTS * capacity) + position)
+        target_ref[k] = base.astype(jnp.int32) + part * capacity
+        weight = row_of(probs_ref[:, k : k + 1])
+        high = weight.astype(BF16).astype(F32)
+        middle = (weight - high).astype(BF16).astype(F32)
+        low = weight - high - middle
+        weight_ref[k] = per_micro(high) + per_micro(middle) + per_micro(low)
 
 
 def per_device(adjoint_out, gate_probs, routes, saved, w_gate, w_up, w_down, probe):
@@ -542,19 +691,26 @@
     wire = PARTS * capacity
     tokens = PARTS * T_MB
     block = CHUNKS * PARTS // replicas * slots
-    target, weight = pick_tables(routes[0], gate_probs[0], capacity)
     order = row_orders(experts, capacity)
     vmem = pl.BlockSpec(memory_space=pltpu.VMEM)
     dma = pltpu.SemaphoreType.DMA
     found = pl.pallas_call(
         functools.partial(relay_kernel, (stages, experts, replicas, capacity)),
         out_shape=jax.ShapeDtypeStruct((model // replicas, width), F32),
-        in_specs=[vmem] * 10,
+        in_specs=[vmem] * 4 + [pl.BlockSpec(memory_space=pl.ANY)] * 6,
         out_specs=vmem,
         scratch_shapes=[
-            pltpu.VMEM((M, TOP, tokens), jnp.int32),
-            pltpu.VMEM((M, TOP, tokens), F32),
-            pltpu.VMEM((M, TOP, tokens), jnp.int32),
+            pltpu.VMEM(adjoint_out.shape, BF16),
+            pltpu.VMEM(saved.shape[3:], BF16),
+            pltpu.VMEM((model, width), BF16),
+            pltpu.VMEM((model, width), BF16),
+            pltpu.VMEM((width, model), BF16),
+            pltpu.VMEM((model, width), BF16),
+            pltpu.VMEM((TOP, M, tokens), jnp.int32),
+            pltpu.VMEM((TOP, M, tokens), F32),
+            pltpu.VMEM((TOP, M, tokens), jnp.int32),
+            pltpu.VMEM((TOP, M, tokens), F32),
+            pltpu.VMEM((TOP, M, tokens), jnp.int32),
             pltpu.VMEM((M, KINDS, CHUNKS, tokens, lanes), BF16),
             pltpu.VMEM((M, KINDS, CHUNKS, tokens, lanes), BF16),
             pltpu.VMEM((M, KINDS, CHUNKS, experts, wire, lanes), BF16),
@@ -572,6 +728,7 @@
             pltpu.VMEM((experts * wire, tokens), BF16),
             pltpu.VMEM((experts * wire, tokens), BF16),
             pltpu.VMEM((experts * wire, lanes), F32),
+            dma((6,)),
             dma((3,)),
             dma((3,)),
             dma((M,)),
@@ -590,8 +747,8 @@
         ),
         name="relay",
     )(
-        target,
-        weight,
+        routes[0],
+        gate_probs[0],
         jnp.asarray(order, BF16),
         jnp.asarray(order.T, BF16),
         adjoint_out,

time: 298 us -> 276 us (0.926)
  Pallas kernels: 291 us -> 270 us
    pallas_call x1, Pallas kernels: 291 us -> 270 us  [per_device(): pl.pallas_call(functools.partial(relay_kernel, (stages, experts, replicas...]
where the time goes in v3:
time: 276 us; the launch traced here: 275 us
  Pallas kernels  270 us (98%)
  local copies, waits for them, and re-layouts  5.08 us (2%)
    pallas_call x1, Pallas kernels, per_device(): pl.pallas_call(functools.partial(relay_kernel, (stages, experts, replicas...  270 us

profile of v3, /device:TPU:1, one launch (start us, length us, event | category | flops | bytes accessed | tf_op | source)
XLA Modules:
  0.0 274.9 jit_solution(10907953382914489441)
XLA Ops:
  0.0 1.4 copy.12
  1.4 1.4 copy.11
  2.8 269.8 %relay.1 = f32[512,512]{1,0:T(8,128)} custom-call(s32[128,2]{1,0:T(8,128)} %bitcast.15, f32[128,2]{1,0:T(8,128)} %bitcast.14, bf16[192,192]{1,0:T(8,128)(2,1)} %constant.4.clone.order_ref, bf16[192,192]{1,0:T(8,128)(2,1)} %constant.5.clone.unorder_ref, bf16[128,2048]{1,0:T(8,128)(2,1)} %adjoint_far.1, bf16[8,4,48,512]{3,2,1,0:T(8,128)(2,1)} %bitcast.13, ...), custom_call_target="tpu_custom_call" | custom-call | tf_op jit(solution)/shard_map/relay/pallas_call | solution.py:697
  272.6 2.3 copy.14

commit v4 on v3

--- a/solution.py
+++ b/solution.py
@@ -315,8 +315,9 @@
                     functools.partial(send_picks, micro, kind, chunk)
                 )
 
-            @pl.when(jnp.logical_not(is_bottom | adds_own))
-            def _():
+        @pl.when(jnp.logical_not(is_bottom | adds_own))
+        def _():
+            for chunk in range(CHUNKS):
                 forward(micro, kind, chunk)
 
     def activations(micro):
@@ -642,11 +643,8 @@
     shift = T_MB.bit_length() - 1
     earlier = (down < across) & ((down >> shift) == (across >> shift))
 
-    def row_of(column):
-        return jnp.sum(jnp.where(same, column, 0.0), axis=0, keepdims=True)
-
-    columns = [routes_ref[:, k : k + 1].astype(F32) for k in range(TOP)]
-    rows = [row_of(column) for column in columns]
+    rows = [routes_ref[k : k + 1, :].astype(F32) for k in range(TOP)]
+    columns = [jnp.sum(jnp.where(same, row, 0.0), axis=1, keepdims=True) for row in rows]
     wide = (M, count)
     own = (lax.broadcasted_iota(jnp.int32, wide, 1) >> shift) == lax.broadcasted_iota(
         jnp.int32, wide, 0
@@ -672,7 +670,7 @@
             position = position + jnp.where(rows[other] == rows[k], 1.0, 0.0)
         base = per_micro(rows[k] * (PARTS * capacity) + position)
         target_ref[k] = base.astype(jnp.int32) + part * capacity
-        weight = row_of(probs_ref[:, k : k + 1])
+        weight = probs_ref[k : k + 1, :]
         high = weight.astype(BF16).astype(F32)
         middle = (weight - high).astype(BF16).astype(F32)
         low = weight - high - middle
@@ -747,8 +745,8 @@
         ),
         name="relay",
     )(
-        routes[0],
-        gate_probs[0],
+        routes[0].T,
+        gate_probs[0].T,
         jnp.asarray(order, BF16),
         jnp.asarray(order.T, BF16),
         adjoint_out,

time: 276 us -> 272 us (0.986)
  local copies, waits for them, and re-layouts: 5.08 us -> 2.26 us
    unnamed x3 -> x1, local copies, waits for them, and re-layouts: 5.08 us -> 2.26 us
where the time goes in v4:
time: 272 us; the launch traced here: 271 us
  Pallas kernels  269 us (99%)
    pallas_call x1, Pallas kernels, per_device(): pl.pallas_call(functools.partial(relay_kernel, (stages, experts, replicas...  269 us

profile of v4, /device:TPU:1, one launch (start us, length us, event | category | flops | bytes accessed | tf_op | source)
XLA Modules:
  0.0 271.5 jit_solution(6800550388054147329)
XLA Ops:
  0.0 269.2 %relay.1 = f32[512,512]{1,0:T(8,128)} custom-call(s32[2,128]{1,0:T(2,128)} %bitcast.18, f32[2,128]{1,0:T(2,128)} %bitcast.19, bf16[192,192]{1,0:T(8,128)(2,1)} %constant.4.clone.order_ref, bf16[192,192]{1,0:T(8,128)(2,1)} %constant.5.clone.unorder_ref, bf16[128,2048]{1,0:T(8,128)(2,1)} %adjoint_far.1, bf16[8,4,48,512]{3,2,1,0:T(8,128)(2,1)} %bitcast.17, ...), custom_call_target="tpu_custom_call" | custom-call | tf_op jit(solution)/shard_map/relay/pallas_call | solution.py:695
  269.2 2.3 copy.12
